TPU v7x, 128 devices: a whole 4x4x4 slice. The times are simulated.
128 devices in a mesh: pts: 32 (over z, y, core), tile: 4 (over x).
Axes of the slice: x: 4, y: 4, z: 4, core: 2. Of those that a mesh axis runs over, the one named last changes fastest.
Arguments:
- values: float32 [128, 64, 1024], P(('pts', 'tile')), may hold values from -6 to 6
- cycle_taps: float32 [128, 64, 8, 1024], P(('pts', 'tile')), may hold values from 0 to 1
- phi_taps: float32 [128, 64, 8, 1024], P(('pts', 'tile')), may hold values from 0 to 1
- cycle_start: int32 [128, 64, 1024], P(('pts', 'tile')), may hold values from 0 to 24
- phi_start: int32 [128, 64, 1024], P(('pts', 'tile')), may hold values from 0 to 248
- tile_list: int32 [128, 32, 2], replicated, may hold values from 0 to 255, as said below
- response: float32 [4097], replicated, may hold values from 0.05 to 1
Outputs:
- filtered_grid: float32 [256, 32, 8192], P(None, 'tile', 'pts')
- gradient: float32 [128, 64, 1024], P(('pts', 'tile'))
Inputs may be any that keep to these rules, and one draw needn't show every extreme that they name: For each point block b and phi column q the 2 entries tile_list[b, q, :] are distinct cycle blocks; slot q * 2 + k of block b holds exactly 1024 points, all of whose taps lie in the tile of cycle block tile_list[b, q, k] and phi column q.
All inputs are finite; a program needn't handle non-finite values.
Results may differ from a plain program's by a relative error of at most 0.0003.
Values sent between devices are 32-bit elements; how exact they have to be, the bound alone decides.
A program may use at most 128 MiB of HBM per device.

v0:
```python
import math

import jax
import jax.numpy as jnp
from jax import lax
from jax.sharding import PartitionSpec as P

NPHI = 8192
TR = 32
NJ = 256
SLOTS_DEV = 64
PPS = 1024


precise = lax.Precision.HIGHEST
radix_first = 64


def contract(formula, lhs_array, rhs_array):
    return jnp.einsum(formula, lhs_array, rhs_array, precision=precise)


def spread_matrix(weights, starts, extent):
    offsets = lax.broadcasted_iota(jnp.int32, (1, 1, extent), 2) - starts[:, :, None]
    result = jnp.zeros(starts.shape + (extent,), jnp.float32)
    for tap_index in range(weights.shape[1]):
        result = result + jnp.where(offsets == tap_index, weights[:, tap_index, :, None], 0.0)
    return result


def angle_table(rows_count, cols_count, modulus):
    left_index = lax.broadcasted_iota(jnp.int32, (rows_count, cols_count), 0)
    right_index = lax.broadcasted_iota(jnp.int32, (rows_count, cols_count), 1)
    phase_int = left_index * right_index % modulus
    angles = phase_int.astype(jnp.float32) * (2.0 * math.pi / modulus)
    return (jnp.cos(angles), jnp.sin(angles))


def filter_cycles(cycle_rows, response):
    length = cycle_rows.shape[-1]
    second = length // radix_first
    cos_first, sin_first = angle_table(radix_first, radix_first, radix_first)
    cos_twist, sin_twist = angle_table(radix_first, second, length)
    cos_second, sin_second = angle_table(second, second, second)
    blocks = cycle_rows.reshape(cycle_rows.shape[:2] + (radix_first, second))
    real_one = contract("giab,ak->gikb", blocks, cos_first)
    imag_one = -contract("giab,ak->gikb", blocks, sin_first)
    real_two = real_one * cos_twist + imag_one * sin_twist
    imag_two = imag_one * cos_twist - real_one * sin_twist
    real_freq = contract("gikb,bm->gikm", real_two, cos_second) + contract(
        "gikb,bm->gikm", imag_two, sin_second
    )
    imag_freq = contract("gikb,bm->gikm", imag_two, cos_second) - contract(
        "gikb,bm->gikm", real_two, sin_second
    )
    full_response = jnp.concatenate([response, response[-2:0:-1]])
    gain_table = full_response.reshape(second, radix_first).T
    real_freq = real_freq * gain_table
    imag_freq = imag_freq * gain_table
    real_back = contract("gikm,bm->gikb", real_freq, cos_second) - contract(
        "gikm,bm->gikb", imag_freq, sin_second
    )
    imag_back = contract("gikm,bm->gikb", imag_freq, cos_second) + contract(
        "gikm,bm->gikb", real_freq, sin_second
    )
    real_turn = real_back * cos_twist - imag_back * sin_twist
    imag_turn = imag_back * cos_twist + real_back * sin_twist
    spatial = contract("gikb,ka->giab", real_turn, cos_first) - contract(
        "gikb,ka->giab", imag_turn, sin_first
    )
    return (spatial / length).reshape(cycle_rows.shape)


def accumulate(arrived, wanted, cycle_blocks):
    selector = (
        lax.broadcasted_iota(jnp.int32, (cycle_blocks, wanted.size), 0) == wanted.reshape(1, -1)
    ).astype(jnp.float32)
    flattened = arrived.reshape(wanted.size, -1)
    return jnp.dot(selector, flattened, precision=precise).reshape(
        (cycle_blocks,) + arrived.shape[2:]
    )


def per_device(values, cycle_taps, phi_taps, cycle_start, phi_start, tile_list, response):
    columns = lax.axis_size("pts")
    part_count = lax.axis_size("tile")
    column = lax.axis_index("pts")
    per_column = SLOTS_DEV // columns
    tile_width = NPHI // columns
    cycle_part = TR // part_count
    cycle_weights = spread_matrix(cycle_taps[0], cycle_start[0], TR)
    phi_weights = spread_matrix(phi_taps[0], phi_start[0], tile_width)
    loaded = cycle_weights * values[0][:, :, None]
    cycle_split = cycle_weights.reshape(columns, per_column, PPS, part_count, cycle_part)
    loaded_split = loaded.reshape(columns, per_column, PPS, part_count, cycle_part)
    phi_split = phi_weights.reshape(columns, per_column, PPS, tile_width)
    partial_value = contract("qkitr,qkic->qtkrc", loaded_split, phi_split)
    partial_value = partial_value.reshape(columns * part_count, per_column, cycle_part, tile_width)
    arrived = lax.all_to_all(
        partial_value, ("pts", "tile"), split_axis=0, concat_axis=0, tiled=True
    )
    wanted = lax.dynamic_index_in_dim(tile_list, column, 1, keepdims=False)
    owned_tiles = accumulate(arrived, wanted, NJ)
    whole_cycles = filter_cycles(
        lax.all_to_all(owned_tiles, "pts", split_axis=0, concat_axis=2, tiled=True), response
    )
    filtered = lax.all_to_all(whole_cycles, "pts", split_axis=2, concat_axis=0, tiled=True)
    picked = jnp.take(filtered, wanted.reshape(-1), axis=0)
    picked = picked.reshape(columns * part_count, per_column, cycle_part, tile_width)
    returned = lax.all_to_all(picked, ("pts", "tile"), split_axis=0, concat_axis=0, tiled=True)
    returned = returned.reshape(columns, part_count, per_column, cycle_part, tile_width)
    rows_read = contract("qkitr,qtkrc->qkic", cycle_split, returned)
    gradient = jnp.sum(rows_read * phi_split, axis=-1).reshape(SLOTS_DEV, PPS)
    return (filtered, gradient[None])


def solution(mesh):
    return jax.shard_map(
        per_device,
        mesh=mesh,
        in_specs=(
            P(("pts", "tile"), None, None),
            P(("pts", "tile"), None, None, None),
            P(("pts", "tile"), None, None, None),
            P(("pts", "tile"), None, None),
            P(("pts", "tile"), None, None),
            P(),
            P(),
        ),
        out_specs=(P(None, "tile", "pts"), P(("pts", "tile"), None, None)),
        check_vma=False,
    )
```

profile of v0, /device:TPU:1, one launch (start us, length us, event | category | flops | bytes accessed | tf_op | source)
XLA Modules:
  0.0 576.5 jit_solution(1086726429451343774)
XLA Ops:
  0.7 13.2 %slice_reduce_fusion.7 = (f32[64,1024]{1,0:T(8,128)S(1)}, f32[64,1024]{1,0:T(8,128)S(1)}, f32[64,1024]{1,0:T(8,128)S(1)}, f32[64,1024]{1,0:T(8,128)S(1)}, f32[64...) fusion(f32[64,8,1024]{2,1,0:T(8,128)} %bitcast.129), kind=kLoop, calls=%fused_computation.64 | loop fusion | bytes 4194304 | tf_op jit(solution)/shard_map/slice | solution.py:27
  15.5 14.8 %slice_reduce_fusion.15 = (f32[64,1024]{1,0:T(8,128)}, f32[64,1024]{1,0:T(8,128)S(1)}, f32[64,1024]{1,0:T(8,128)S(1)}, f32[64,1024]{1,0:T(8,128)S(1)}, f32[64,10...) fusion(f32[64,8,1024]{2,1,0:T(8,128)} %bitcast.130), kind=kLoop, calls=%fused_computation.72 | loop fusion | bytes 4194304 | tf_op jit(solution)/shard_map/slice | solution.py:27
  43.8 7.6 %fusion.177 = f32[32,2,1024,32]{2,3,1,0:T(8,128)S(1)} fusion(f32[32,2,1024]{2,1,0:T(2,128)S(1)} %mul.208, f32[32,2,1024]{2,1,0:T(2,128)S(1)} %broadcast_in_dim.192, f32[32,2,1024]{2,1,0:T(2,128)S(1)} %broadcast_in_dim.190, f32[32,2,1024]{2,1,0:T(2,128)S(1)} %broadcast_in_dim.188, f32[32,2,1024]{2,1,0:T(2,128)S(1)} %broadcast_in_dim.186, ...), kind=kLoop, calls=%fused_computation.22.clone.clone.clone.2 | loop fusion | flops 52428800 | bytes 11010176
  51.5 118.1 %fusion.36 = f32[32,4,2,8,256]{4,3,1,2,0:T(8,128)S(1)} fusion(f32[32,2,1024]{2,1,0:T(2,128)S(1)} %copy-done.30, f32[32,2,1024]{2,1,0:T(2,128)S(1)} %copy-done.29, f32[32,2,1024]{2,1,0:T(2,128)S(1)} %copy-done.28, f32[32,2,1024]{2,1,0:T(2,128)S(1)} %copy-done.27, f32[32,2,1024]{2,1,0:T(2,128)S(1)} %copy-done.25, f32[32,2,1024]{2,1,0:T(2,128)S(1)} %copy-done.24, ...), kind=kOutput, calls=%fused_computation.51 | convolution fusion | flops 6845104128 | bytes 12845056
  171.2 11.5 %all-to-all-start = ((f32[128,2,8,256]{3,2,1,0:T(8,128)}), f32[128,2,8,256]{3,2,1,0:T(8,128)S(1)}, u32[]{:S(2)}, u32[]{:S(2)}) async-start(f32[128,2,8,256]{3,2,1,0:T(8,128)} %bitcast.125), calls=%async_computation | async-start | bytes 4194304 | tf_op jit(solution)/shard_map/all_to_all | solution.py:99
  183.7 29.8 %all-to-all-done = f32[128,2,8,256]{3,2,1,0:T(8,128)S(1)} async-done(((f32[128,2,8,256]{3,2,1,0:T(8,128)}), f32[128,2,8,256]{3,2,1,0:T(8,128)S(1)}, u32[]{:S(2)}, u32[]{:S(2)}) %all-to-all-start) | async-done | bytes 2097184 | tf_op jit(solution)/shard_map/all_to_all | solution.py:99
  213.5 2.2 copy.63
  218.9 2.5 copy.32
  221.4 4.1 all-to-all-start.1
  226.2 27.7 %all-to-all-done.1 = f32[256,8,256]{2,1,0:T(8,128)S(1)} async-done(((f32[256,8,256]{2,1,0:T(8,128)}), f32[256,8,256]{2,1,0:T(8,128)S(1)}, u32[]{:S(2)}, u32[]{:S(2)}) %all-to-all-start.1) | async-done | bytes 2097184 | tf_op jit(solution)/shard_map/all_to_all | solution.py:105
  253.8 2.5 copy.68
  262.6 2.2 fusion.13
  264.8 2.2 fusion.15
  267.1 2.3 subtract_multiply_fusion
  269.3 2.3 fusion.54
  271.6 2.2 add_multiply_fusion
  276.0 2.1 convolution_add_fusion
  278.1 2.1 convolution_subtract_fusion
  282.3 2.2 multiply_bitcast_fusion
  284.5 13.9 %copy.46 = f32[8,8,64,128]{1,0,3,2:T(8,128)} copy(f32[8,8,64,128]{3,2,1,0:T(8,128)S(1)} %multiply_bitcast_fusion) | data formatting | bytes 4194304 | tf_op jit(solution)/shard_map/reshape | solution.py:71
  298.3 24.3 %reshape.216 = f32[32,1,16384]{2,1,0:T(1,128)} reshape(f32[8192,8,8]{2,1,0:T(8,128)} %bitcast.118) | data formatting | bytes 4194304
  322.6 6.3 %all-to-all-start.2 = ((f32[32,1,16384]{2,1,0:T(1,128)}), f32[32,1,16384]{2,1,0:T(1,128)S(1)}, u32[]{:S(2)}, u32[]{:S(2)}) async-start(f32[32,1,16384]{2,1,0:T(1,128)} %reshape.216), calls=%async_computation.2 | async-start | bytes 4194304 | tf_op jit(solution)/shard_map/all_to_all | solution.py:107
  329.3 28.2 %all-to-all-done.2 = f32[32,1,16384]{2,1,0:T(1,128)S(1)} async-done(((f32[32,1,16384]{2,1,0:T(1,128)}), f32[32,1,16384]{2,1,0:T(1,128)S(1)}, u32[]{:S(2)}, u32[]{:S(2)}) %all-to-all-start.2) | async-done | bytes 2097184 | tf_op jit(solution)/shard_map/all_to_all | solution.py:107
  359.4 7.4 %reduce.32 = f32[32,16384]{1,0:T(8,128)S(1)} reduce(f32[32,1,16384]{2,1,0:T(1,128)} %copy-done.1, f32[]{:T(128)} %broadcast.251), dimensions={1}, to_apply=%all_to_all.34.reduce_sub_computation | reduce | bytes 4194308 | tf_op jit(solution)/shard_map/all_to_all | solution.py:107
  366.8 31.1 %reshape.217 = f32[8192,8,8]{2,1,0:T(8,128)} reshape(f32[32,16384]{1,0:T(8,128)S(1)} %reduce.32) | data formatting | bytes 4194304
  397.9 18.6 %copy.36 = f32[32,8,8,256]{3,2,1,0:T(8,128)S(1)} copy(f32[32,8,8,256]{2,1,3,0:T(8,128)} %bitcast.119) | data formatting | bytes 4194304 | tf_op jit(solution)/shard_map/all_to_all | solution.py:107
  416.5 2.4 gather_fusion
  418.9 3.2 broadcast_select_fusion
  422.2 6.4 %all-to-all-start.3 = ((f32[128,2,8,256]{3,2,1,0:T(8,128)}), f32[128,2,8,256]{3,2,1,0:T(8,128)}, u32[]{:S(2)}, u32[]{:S(2)}) async-start(f32[128,2,8,256]{3,2,1,0:T(8,128)} %broadcast_select_fusion), calls=%async_computation.3 | async-start | bytes 4194304 | tf_op jit(solution)/shard_map/all_to_all | solution.py:110
  428.7 8.6 %select_add_fusion.12 = f32[32,2,1024,4,8]{2,4,3,1,0:T(8,128)} fusion(f32[32,2,1024]{2,1,0:T(2,128)S(1)} %copy-done.17, f32[32,2,1024]{2,1,0:T(2,128)S(1)} %copy-done.15, f32[32,2,1024]{2,1,0:T(2,128)S(1)} %copy-done.13, f32[32,2,1024]{2,1,0:T(2,128)S(1)} %copy-done.11, f32[32,2,1024]{2,1,0:T(2,128)S(1)} %copy-done.9, ...), kind=kLoop, calls=%fused_computation.24.clone.clone.1 | loop fusion | flops 50331648 | bytes 10748032 | tf_op jit(solution)/shard_map/qkitr,qtkrc->qkic/dot_general | solution.py:20
  437.3 21.9 %all-to-all-done.3 = f32[128,2,8,256]{3,2,1,0:T(8,128)} async-done(((f32[128,2,8,256]{3,2,1,0:T(8,128)}), f32[128,2,8,256]{3,2,1,0:T(8,128)}, u32[]{:S(2)}, u32[]{:S(2)}) %all-to-all-start.3) | async-done | bytes 2097184 | tf_op jit(solution)/shard_map/all_to_all | solution.py:110
  459.2 116.3 %fusion = f32[32,2,1024]{2,1,0:T(2,128)S(1)} fusion(f32[32,2,1024]{2,1,0:T(2,128)} %broadcast_in_dim.175, f32[32,2,1024]{2,1,0:T(2,128)} %broadcast_in_dim.173, f32[32,2,1024]{2,1,0:T(2,128)} %broadcast_in_dim.171, f32[32,2,1024]{2,1,0:T(2,128)} %broadcast_in_dim.169, f32[32,2,1024]{2,1,0:T(2,128)S(1)} %copy-done.26, f32[32,2,1024]{2,1,0:T(2,128)S(1)} %copy-done.24, ...), kind=kOutput, calls=%fused_computation.2 | convolution fusion | flops 6878593024 | bytes 13107200 | tf_op jit(solution)/shard_map/qkitr,qtkrc->qkic/dot_general | solution.py:20
  (114 shorter events, 34.7 us)
Async XLA Ops:
  0.6 43.0 %copy-start.33 = (s32[4,8]{1,0:T(4,128)}, s32[4,8]{1,0:T(4,128)S(1)}, u32[]{:S(2)}) copy-start(s32[4,8]{1,0:T(4,128)S(1)} %multiply_add_fusion.3) | copy-start | bytes 388
  14.0 29.6 %copy-start.2 = (f32[32,2,1024]{2,1,0:T(2,128)}, f32[32,2,1024]{2,1,0:T(2,128)S(1)}, u32[]{:S(2)}) copy-start(f32[32,2,1024]{2,1,0:T(2,128)S(1)} %broadcast_in_dim.177) | copy-start | bytes 786436
  14.2 29.5 %copy-start.4 = (f32[32,2,1024]{2,1,0:T(2,128)}, f32[32,2,1024]{2,1,0:T(2,128)S(1)}, u32[]{:S(2)}) copy-start(f32[32,2,1024]{2,1,0:T(2,128)S(1)} %broadcast_in_dim.180) | copy-start | bytes 786436
  14.4 29.3 %copy-start.6 = (f32[32,2,1024]{2,1,0:T(2,128)}, f32[32,2,1024]{2,1,0:T(2,128)S(1)}, u32[]{:S(2)}) copy-start(f32[32,2,1024]{2,1,0:T(2,128)S(1)} %broadcast_in_dim.182) | copy-start | bytes 786436
  14.5 29.1 %copy-start.8 = (f32[32,2,1024]{2,1,0:T(2,128)}, f32[32,2,1024]{2,1,0:T(2,128)S(1)}, u32[]{:S(2)}) copy-start(f32[32,2,1024]{2,1,0:T(2,128)S(1)} %broadcast_in_dim.184) | copy-start | bytes 786436
  14.7 29.0 %copy-start.10 = (f32[32,2,1024]{2,1,0:T(2,128)}, f32[32,2,1024]{2,1,0:T(2,128)S(1)}, u32[]{:S(2)}) copy-start(f32[32,2,1024]{2,1,0:T(2,128)S(1)} %broadcast_in_dim.186) | copy-start | bytes 786436
  14.9 28.8 %copy-start.12 = (f32[32,2,1024]{2,1,0:T(2,128)}, f32[32,2,1024]{2,1,0:T(2,128)S(1)}, u32[]{:S(2)}) copy-start(f32[32,2,1024]{2,1,0:T(2,128)S(1)} %broadcast_in_dim.188) | copy-start | bytes 786436
  15.0 28.7 %copy-start.14 = (f32[32,2,1024]{2,1,0:T(2,128)}, f32[32,2,1024]{2,1,0:T(2,128)S(1)}, u32[]{:S(2)}) copy-start(f32[32,2,1024]{2,1,0:T(2,128)S(1)} %broadcast_in_dim.190) | copy-start | bytes 786436
  15.2 28.5 %copy-start.16 = (f32[32,2,1024]{2,1,0:T(2,128)}, f32[32,2,1024]{2,1,0:T(2,128)S(1)}, u32[]{:S(2)}) copy-start(f32[32,2,1024]{2,1,0:T(2,128)S(1)} %broadcast_in_dim.192) | copy-start | bytes 786436
  15.4 28.3 %copy-start.18 = (s32[32,2,1024]{2,1,0:T(2,128)}, s32[32,2,1024]{2,1,0:T(2,128)S(1)}, u32[]{:S(2)}) copy-start(s32[32,2,1024]{2,1,0:T(2,128)S(1)} %sub.66) | copy-start | bytes 786436
  43.7 7.7 %copy-start.22 = (f32[32,2,1024]{2,1,0:T(2,128)S(1)}, f32[32,2,1024]{2,1,0:T(2,128)}, u32[]{:S(2)}) copy-start(f32[32,2,1024]{2,1,0:T(2,128)} %broadcast_in_dim.160) | copy-start | bytes 786436
  43.7 7.7 %copy-start.23 = (f32[32,2,1024]{2,1,0:T(2,128)S(1)}, f32[32,2,1024]{2,1,0:T(2,128)}, u32[]{:S(2)}) copy-start(f32[32,2,1024]{2,1,0:T(2,128)} %broadcast_in_dim.163) | copy-start | bytes 786436
  43.7 7.7 %copy-start.24 = (f32[32,2,1024]{2,1,0:T(2,128)S(1)}, f32[32,2,1024]{2,1,0:T(2,128)}, u32[]{:S(2)}) copy-start(f32[32,2,1024]{2,1,0:T(2,128)} %broadcast_in_dim.165) | copy-start | bytes 786436
  43.7 7.7 %copy-start.25 = (f32[32,2,1024]{2,1,0:T(2,128)S(1)}, f32[32,2,1024]{2,1,0:T(2,128)}, u32[]{:S(2)}) copy-start(f32[32,2,1024]{2,1,0:T(2,128)} %broadcast_in_dim.167) | copy-start | bytes 786436
  43.8 7.7 %copy-start.27 = (f32[32,2,1024]{2,1,0:T(2,128)S(1)}, f32[32,2,1024]{2,1,0:T(2,128)}, u32[]{:S(2)}) copy-start(f32[32,2,1024]{2,1,0:T(2,128)} %broadcast_in_dim.169) | copy-start | bytes 786436
  43.8 7.7 %copy-start.28 = (f32[32,2,1024]{2,1,0:T(2,128)S(1)}, f32[32,2,1024]{2,1,0:T(2,128)}, u32[]{:S(2)}) copy-start(f32[32,2,1024]{2,1,0:T(2,128)} %broadcast_in_dim.171) | copy-start | bytes 786436
  43.8 7.7 %copy-start.29 = (f32[32,2,1024]{2,1,0:T(2,128)S(1)}, f32[32,2,1024]{2,1,0:T(2,128)}, u32[]{:S(2)}) copy-start(f32[32,2,1024]{2,1,0:T(2,128)} %broadcast_in_dim.173) | copy-start | bytes 786436
  43.8 7.7 %copy-start.30 = (f32[32,2,1024]{2,1,0:T(2,128)S(1)}, f32[32,2,1024]{2,1,0:T(2,128)}, u32[]{:S(2)}) copy-start(f32[32,2,1024]{2,1,0:T(2,128)} %broadcast_in_dim.175) | copy-start | bytes 786436
  43.8 7.7 %copy-start.31 = (s32[32,2,1024]{2,1,0:T(2,128)S(1)}, s32[32,2,1024]{2,1,0:T(2,128)}, u32[]{:S(2)}) copy-start(s32[32,2,1024]{2,1,0:T(2,128)} %sub.59) | copy-start | bytes 786436
  171.2 42.3 %all-to-all-start = ((f32[128,2,8,256]{3,2,1,0:T(8,128)}), f32[128,2,8,256]{3,2,1,0:T(8,128)S(1)}, u32[]{:S(2)}, u32[]{:S(2)}) async-start(f32[128,2,8,256]{3,2,1,0:T(8,128)} %bitcast.125), calls=%async_computation | async-start | bytes 4194304 | tf_op jit(solution)/shard_map/all_to_all | solution.py:99
  221.4 32.5 %all-to-all-start.1 = ((f32[256,8,256]{2,1,0:T(8,128)}), f32[256,8,256]{2,1,0:T(8,128)S(1)}, u32[]{:S(2)}, u32[]{:S(2)}) async-start(f32[256,8,256]{2,1,0:T(8,128)} %copy.32), calls=%async_computation.1 | async-start | bytes 4194304 | tf_op jit(solution)/shard_map/all_to_all | solution.py:105
  322.6 34.8 %all-to-all-start.2 = ((f32[32,1,16384]{2,1,0:T(1,128)}), f32[32,1,16384]{2,1,0:T(1,128)S(1)}, u32[]{:S(2)}, u32[]{:S(2)}) async-start(f32[32,1,16384]{2,1,0:T(1,128)} %reshape.216), calls=%async_computation.2 | async-start | bytes 4194304 | tf_op jit(solution)/shard_map/all_to_all | solution.py:107
  422.1 6.5 %copy-start.7 = (f32[32,2,1024]{2,1,0:T(2,128)S(1)}, f32[32,2,1024]{2,1,0:T(2,128)}, u32[]{:S(2)}) copy-start(f32[32,2,1024]{2,1,0:T(2,128)} %copy-done.6) | copy-start | bytes 786436
  422.1 6.5 %copy-start.9 = (f32[32,2,1024]{2,1,0:T(2,128)S(1)}, f32[32,2,1024]{2,1,0:T(2,128)}, u32[]{:S(2)}) copy-start(f32[32,2,1024]{2,1,0:T(2,128)} %copy-done.8) | copy-start | bytes 786436
  422.1 6.5 %copy-start.11 = (f32[32,2,1024]{2,1,0:T(2,128)S(1)}, f32[32,2,1024]{2,1,0:T(2,128)}, u32[]{:S(2)}) copy-start(f32[32,2,1024]{2,1,0:T(2,128)} %copy-done.10) | copy-start | bytes 786436
  422.1 6.5 %copy-start.13 = (f32[32,2,1024]{2,1,0:T(2,128)S(1)}, f32[32,2,1024]{2,1,0:T(2,128)}, u32[]{:S(2)}) copy-start(f32[32,2,1024]{2,1,0:T(2,128)} %copy-done.12) | copy-start | bytes 786436
  422.1 6.5 %copy-start.15 = (f32[32,2,1024]{2,1,0:T(2,128)S(1)}, f32[32,2,1024]{2,1,0:T(2,128)}, u32[]{:S(2)}) copy-start(f32[32,2,1024]{2,1,0:T(2,128)} %copy-done.14) | copy-start | bytes 786436
  422.1 6.5 %copy-start.17 = (f32[32,2,1024]{2,1,0:T(2,128)S(1)}, f32[32,2,1024]{2,1,0:T(2,128)}, u32[]{:S(2)}) copy-start(f32[32,2,1024]{2,1,0:T(2,128)} %copy-done.16) | copy-start | bytes 786436
  422.2 6.5 %copy-start.19 = (s32[32,2,1024]{2,1,0:T(2,128)S(1)}, s32[32,2,1024]{2,1,0:T(2,128)}, u32[]{:S(2)}) copy-start(s32[32,2,1024]{2,1,0:T(2,128)} %copy-done.18) | copy-start | bytes 786436
  422.2 6.5 %copy-start.34 = (s32[4,8]{1,0:T(4,128)S(1)}, s32[4,8]{1,0:T(4,128)}, u32[]{:S(2)}) copy-start(s32[4,8]{1,0:T(4,128)} %copy-done.33) | copy-start | bytes 388
  422.2 37.0 %all-to-all-start.3 = ((f32[128,2,8,256]{3,2,1,0:T(8,128)}), f32[128,2,8,256]{3,2,1,0:T(8,128)}, u32[]{:S(2)}, u32[]{:S(2)}) async-start(f32[128,2,8,256]{3,2,1,0:T(8,128)} %broadcast_select_fusion), calls=%async_computation.3 | async-start | bytes 4194304 | tf_op jit(solution)/shard_map/all_to_all | solution.py:110
  428.7 30.4 %copy-start.26 = (f32[32,2,1024]{2,1,0:T(2,128)S(1)}, f32[32,2,1024]{2,1,0:T(2,128)}, u32[]{:S(2)}) copy-start(f32[32,2,1024]{2,1,0:T(2,128)} %broadcast_in_dim.167) | copy-start | bytes 786436
  (7 other events, 23.6 us)
where the time goes:
time: 586 us; the launch traced here: 577 us
  matrix products  262 us (45%)
  local copies, waits for them, and re-layouts  150 us (26%)
  waiting for transfers between devices  108 us (18%)
  starting transfers between devices  28.4 us (5%)
  other arithmetic  27.8 us (5%)
    dot_general x13, matrix products, contract(): return jnp.einsum(formula, lhs_array, rhs_array, precision=precise)  142 us
    unnamed x1, matrix products  118 us
    unnamed x75, local copies, waits for them, and re-layouts  59.1 us
    all_to_all x1, waiting for transfers between devices, per_device(): lax.all_to_all(partial_value, ('pts', 'tile'), split_axis=0, concat_axis=...  29.8 us
    all_to_all x1, waiting for transfers between devices, per_device(): lax.all_to_all(whole_cycles, 'pts', split_axis=2, concat_axis=0, tiled=True)  28.2 us
    slice x2, local copies, waits for them, and re-layouts, spread_matrix(): weights[:, tap_index, :, None]  27.9 us
    all_to_all x1, waiting for transfers between devices, per_device(): lax.all_to_all(owned_tiles, 'pts', split_axis=0, concat_axis=2, tiled=True)  27.7 us
    all_to_all x1, waiting for transfers between devices, per_device(): lax.all_to_all(picked, ('pts', 'tile'), split_axis=0, concat_axis=0, tile...  21.9 us
  transfers between devices with their start and end apart: 4, of which 4 were waited for; matrix products, arithmetic and copies ran while one was open for 2% of the time, Pallas kernels for 0%

commit v1 on v0

v1 whole, which is shorter than its diff:
```python
import functools
import math

import jax
import jax.numpy as jnp
import numpy as np
from jax import lax
from jax.experimental import pallas as pl
from jax.experimental.pallas import tpu as pltpu
from jax.sharding import PartitionSpec as P

NPHI = 8192
TR = 32
NJ = 256
TP = 256
PPS = 1024
COLS = 32
SLOTS_DEV = 64
HALF = COLS // 2 + 1

F32 = jnp.float32
BF16 = jnp.bfloat16
CONTRACT_LAST = (((1,), (1,)), ((), ()))


def split(x):
    high = x.astype(BF16)
    return high, (x - high.astype(F32)).astype(BF16)


def place(taps, start):
    count = taps.shape[1]
    row = lax.broadcasted_iota(jnp.int32, (8, count), 0)
    starts = jnp.broadcast_to(start, (8, count))
    for bit in (1, 2, 4):
        taps = jnp.where((starts & bit) != 0, pltpu.roll(taps, bit, 0), taps)
    return taps, (starts - row + 7) >> 3


def expand(parts, group, groups):
    group = group.astype(F32)
    count = group.shape[1]
    pair = jnp.concatenate([group, group - 1.0], 0).astype(BF16)
    doubled = [jnp.concatenate([part.astype(F32)] * 2, 0).astype(BF16) for part in parts]
    zero = jnp.zeros((16, count), BF16)
    rows = [[] for _ in parts]
    for index in range(groups // 2):
        mask = pair == jnp.asarray(2 * index, BF16)
        for out, part in zip(rows, doubled):
            out.append(jnp.where(mask, part, zero))
    return [jnp.concatenate(out, 0) for out in rows]


def spread_kernel(v_ref, ct_ref, pt_ref, cs_ref, ps_ref, o_ref):
    for s in range(v_ref.shape[0]):
        cycle, cycle_group = place(ct_ref[s] * v_ref[s : s + 1, :], cs_ref[s : s + 1, :])
        phi, phi_group = place(pt_ref[s], ps_ref[s : s + 1, :])
        cycle_high, cycle_low = expand(split(cycle), cycle_group, TR // 8)
        phi_high, phi_low = expand(split(phi), phi_group, TP // 8)
        stacked = jnp.concatenate([cycle_high, cycle_low], 0)
        first = lax.dot_general(phi_high, stacked, CONTRACT_LAST, preferred_element_type=F32)
        second = lax.dot_general(phi_low, cycle_high, CONTRACT_LAST, preferred_element_type=F32)
        tile = (first[:, :TR] + first[:, TR:] + second).T
        o_ref[s // 2, :, s % 2] = tile.reshape(4, 8, TP)


def spread(values, cycle_taps, phi_taps, cycle_start, phi_start, block=8):
    slots = values.shape[0]
    flat = pl.BlockSpec((block, PPS), lambda i: (i, 0))
    taps = pl.BlockSpec((block, 8, PPS), lambda i: (i, 0, 0))
    return pl.pallas_call(
        spread_kernel,
        grid=(slots // block,),
        in_specs=[flat, taps, taps, flat, flat],
        out_specs=pl.BlockSpec((block // 2, 4, 2, 8, TP), lambda i: (i, 0, 0, 0, 0)),
        out_shape=jax.ShapeDtypeStruct((slots // 2, 4, 2, 8, TP), F32),
        name="spread",
    )(values, cycle_taps, phi_taps, cycle_start, phi_start)


def read_kernel(f_ref, ct_ref, pt_ref, cs_ref, ps_ref, o_ref):
    rows = []
    for s in range(ct_ref.shape[0]):
        tile_high, tile_low = split(f_ref[s // 2, :, s % 2].reshape(TR, TP))
        cycle, cycle_group = place(ct_ref[s], cs_ref[s : s + 1, :])
        phi, phi_group = place(pt_ref[s], ps_ref[s : s + 1, :])
        cycle_high, cycle_low = expand(split(cycle), cycle_group, TR // 8)
        right = jnp.concatenate([cycle_high, cycle_low, cycle_high], 0)
        left = jnp.concatenate([tile_high, tile_high, tile_low], 0).T
        along = jnp.dot(left, right, preferred_element_type=F32)
        picked = jnp.zeros((8, PPS), F32)
        for g in range(TP // 8):
            picked = jnp.where(phi_group == g, along[8 * g : 8 * g + 8], picked)
        rows.append(jnp.sum(picked * phi, 0, keepdims=True))
    o_ref[...] = jnp.concatenate(rows, 0)


def read_back(tiles, cycle_taps, phi_taps, cycle_start, phi_start, block=8):
    slots = cycle_taps.shape[0]
    flat = pl.BlockSpec((block, PPS), lambda i: (i, 0))
    taps = pl.BlockSpec((block, 8, PPS), lambda i: (i, 0, 0))
    return pl.pallas_call(
        read_kernel,
        grid=(slots // block,),
        in_specs=[
            pl.BlockSpec((block // 2, 4, 2, 8, TP), lambda i: (i, 0, 0, 0, 0)),
            taps,
            taps,
            flat,
            flat,
        ],
        out_specs=flat,
        out_shape=jax.ShapeDtypeStruct((slots, PPS), F32),
        name="read_back",
    )(tiles, cycle_taps, phi_taps, cycle_start, phi_start)


def accumulate_kernel(j_ref, a_ref, o_ref):
    o_ref[...] = jnp.zeros_like(o_ref)

    def step(i, carry):
        j = j_ref[i]
        o_ref[j] = o_ref[j] + a_ref[i]
        return carry

    lax.fori_loop(0, a_ref.shape[0], step, 0, unroll=8)


def pick_kernel(j_ref, f_ref, o_ref):
    def step(i, carry):
        o_ref[i] = f_ref[j_ref[i]]
        return carry

    lax.fori_loop(0, o_ref.shape[0], step, 0, unroll=8)


def by_index(kernel, name, index, tiles, count):
    vmem = pl.BlockSpec(memory_space=pltpu.VMEM)
    return pl.pallas_call(
        kernel,
        in_specs=[pl.BlockSpec(memory_space=pltpu.SMEM), vmem],
        out_specs=vmem,
        out_shape=jax.ShapeDtypeStruct((count,) + tiles.shape[1:], F32),
        name=name,
    )(index, tiles)


def times(re, im, cos, sin):
    return re * cos - im * sin, re * sin + im * cos


def turn(re, im, angle):
    cos, sin = math.cos(angle), math.sin(angle)
    if abs(sin) < 1e-12:
        return (re, im) if cos > 0 else (-re, -im)
    if abs(cos) < 1e-12:
        return (-im, re) if sin > 0 else (im, -re)
    return re * cos - im * sin, re * sin + im * cos


def real_fft(x):
    n = len(x)
    if n == 1:
        return [(x[0], None)]
    if n == 2:
        return [(x[0] + x[1], None), (x[0] - x[1], None)]
    even, odd = real_fft(x[0::2]), real_fft(x[1::2])
    out = [None] * (n // 2 + 1)
    out[0] = (even[0][0] + odd[0][0], None)
    out[n // 2] = (even[0][0] - odd[0][0], None)
    for k in range(1, n // 4):
        er, ei = even[k]
        tr, ti = turn(odd[k][0], odd[k][1], -2.0 * math.pi * k / n)
        out[k] = (er + tr, ei + ti)
        out[n // 2 - k] = (er - tr, ti - ei)
    quarter = n // 4
    out[quarter] = (even[quarter][0], -odd[quarter][0])
    return out


def real_inverse(spec):
    half = len(spec) - 1
    n = 2 * half
    if n == 2:
        return [spec[0][0] + spec[1][0], spec[0][0] - spec[1][0]]
    even, odd = [None] * (half // 2 + 1), [None] * (half // 2 + 1)
    even[0] = (spec[0][0] + spec[half][0], None)
    odd[0] = (spec[0][0] - spec[half][0], None)
    for k in range(1, half // 2):
        ar, ai = spec[k]
        br, bi = spec[half - k]
        even[k] = (ar + br, ai - bi)
        odd[k] = turn(ar - br, ai + bi, 2.0 * math.pi * k / n)
    middle = half // 2
    even[middle] = (2.0 * spec[middle][0], None)
    odd[middle] = (-2.0 * spec[middle][1], None)
    out = [None] * n
    out[0::2] = real_inverse(even)
    out[1::2] = real_inverse(odd)
    return out


def times_table(rows, table_high, table_low):
    high, low = split(rows)
    dot = functools.partial(jnp.dot, preferred_element_type=F32)
    return dot(high, table_high) + dot(high, table_low) + dot(low, table_high)


def filter_kernel(x_ref, gain_ref, twist_ref, high_ref, low_ref, o_ref):
    cycles = x_ref.shape[1]
    spec = real_fft([x_ref[q] for q in range(COLS)])
    reals, imags = [], []
    for k in range(HALF):
        cos, sin = twist_ref[0, k : k + 1, :], twist_ref[1, k : k + 1, :]
        re, im = spec[k]
        if im is None:
            reals.append(re * cos)
            imags.append(-re * sin)
        else:
            re, im = times(re, im, cos, -sin)
            reals.append(re)
            imags.append(im)
    count = HALF * cycles
    both = times_table(jnp.concatenate(reals + imags, 0), high_ref[...], low_ref[...])
    first, last = both[:count], both[count:]
    freq_re = first[:, :TP] + last[:, TP:]
    freq_im = last[:, :TP] - first[:, TP:]
    gains = [jnp.broadcast_to(gain_ref[k : k + 1, :], (cycles, TP)) for k in range(HALF)]
    gain = jnp.concatenate(gains, 0)
    both = times_table(
        jnp.concatenate([freq_re * gain, freq_im * gain], 0), high_ref[...], low_ref[...]
    )
    first, last = both[:count], both[count:]
    back_re = first[:, :TP] - last[:, TP:]
    back_im = last[:, :TP] + first[:, TP:]
    spec = []
    for k in range(HALF):
        cos, sin = twist_ref[0, k : k + 1, :], twist_ref[1, k : k + 1, :]
        re, im = back_re[k * cycles : (k + 1) * cycles], back_im[k * cycles : (k + 1) * cycles]
        spec.append(times(re, im, cos, sin))
    for q, row in enumerate(real_inverse(spec)):
        o_ref[q] = row


def filter_tables():
    index = np.arange(TP)
    angle = 2.0 * np.pi * (np.outer(index, index) % TP) / TP
    table = np.concatenate([np.cos(angle), np.sin(angle)], 1).astype(np.float32)
    high = table.astype(BF16)
    low = (table - high.astype(np.float32)).astype(BF16)
    angle = 2.0 * np.pi * np.outer(np.arange(HALF), index) / NPHI
    return np.stack([np.cos(angle), np.sin(angle)]).astype(np.float32), high, low


def filter_cycles(cycles, response, block=16):
    count = cycles.shape[1]
    full = jnp.concatenate([response, response[-2:0:-1]]) * (1.0 / NPHI)
    gain = full.reshape(TP, COLS).T[:HALF]
    twist, high, low = filter_tables()
    spec = pl.BlockSpec((COLS, block, TP), lambda i: (0, i, 0))
    whole = lambda *shape: pl.BlockSpec(shape, lambda i: (0,) * len(shape))
    return pl.pallas_call(
        filter_kernel,
        grid=(count // block,),
        in_specs=[spec, whole(HALF, TP), whole(2, HALF, TP), whole(TP, 2 * TP), whole(TP, 2 * TP)],
        out_specs=spec,
        out_shape=jax.ShapeDtypeStruct(cycles.shape, F32),
        name="filter",
    )(cycles, gain, jnp.asarray(twist), jnp.asarray(high), jnp.asarray(low))


def per_device(values, cycle_taps, phi_taps, cycle_start, phi_start, tile_list, response):
    column = lax.axis_index("pts")
    part_count = lax.axis_size("tile")
    points = (cycle_taps[0], phi_taps[0], cycle_start[0], phi_start[0])
    partial = spread(values[0], *points).reshape(COLS * part_count, 2, 8, TP)
    arrived = lax.all_to_all(partial, ("pts", "tile"), split_axis=0, concat_axis=0, tiled=True)
    wanted = lax.dynamic_index_in_dim(tile_list, column, 1, keepdims=False).reshape(-1)
    owned = by_index(accumulate_kernel, "accumulate", wanted, arrived.reshape(-1, 8, TP), NJ)
    cycles = lax.all_to_all(owned, "pts", split_axis=0, concat_axis=0, tiled=True)
    whole = filter_cycles(cycles.reshape(COLS, -1, TP), response)
    filtered = lax.all_to_all(whole, "pts", split_axis=0, concat_axis=0, tiled=True)
    filtered = filtered.reshape(NJ, 8, TP)
    picked = by_index(pick_kernel, "pick", wanted, filtered, wanted.size)
    picked = picked.reshape(COLS * part_count, 2, 8, TP)
    returned = lax.all_to_all(picked, ("pts", "tile"), split_axis=0, concat_axis=0, tiled=True)
    gradient = read_back(returned.reshape(COLS, part_count, 2, 8, TP), *points)
    return filtered, gradient[None]


def solution(mesh):
    return jax.shard_map(
        per_device,
        mesh=mesh,
        in_specs=(
            P(("pts", "tile"), None, None),
            P(("pts", "tile"), None, None, None),
            P(("pts", "tile"), None, None, None),
            P(("pts", "tile"), None, None),
            P(("pts", "tile"), None, None),
            P(),
            P(),
        ),
        out_specs=(P(None, "tile", "pts"), P(("pts", "tile"), None, None)),
        check_vma=False,
    )
```

time: 586 us -> 203 us (0.35); the launches traced: 577 us -> 202 us
  matrix products: 262 us -> 0 us
  local copies, waits for them, and re-layouts: 150 us -> 5.79 us
  blocking collectives: 0 us -> 70.6 us
  Pallas kernels: 0 us -> 52.3 us
  waiting for transfers between devices: 108 us -> 57.1 us
  other arithmetic: 27.8 us -> 0.08 us
  starting transfers between devices: 28.4 us -> 15.6 us
    dot_general x14 -> x0, matrix products: 143 us -> none  [the longest x13 142 us: contract(): return jnp.einsum(formula, lhs_array, rhs_array, precision=precise)]
    unnamed x1 -> x0, matrix products: 118 us -> none
    all_to_all x0 -> x2, blocking collectives: none -> 70.6 us  [the longest x1 35.7 us: per_device(): lax.all_to_all(picked, ('pts', 'tile'), split_axis=0, concat_axis=0, tile...]
    unnamed x75 -> x13, local copies, waits for them, and re-layouts: 59.1 us -> 4.13 us
    pallas_call x0 -> x5, Pallas kernels: none -> 52.3 us  [the longest x1 21.5 us: spread(): pl.pallas_call(spread_kernel, grid=(slots // block,), in_specs=[flat, tap...]
    all_to_all x4 -> x2, waiting for transfers between devices: 108 us -> 57.1 us  [the longest x1 29.9 us: per_device(): lax.all_to_all(partial, ('pts', 'tile'), split_axis=0, concat_axis=0, til...]
    slice x3 -> x2, local copies, waits for them, and re-layouts: 28 us -> 0.7 us  [the longest x1 0.62 us: filter_cycles(): gain = full.reshape(TP, COLS).T[:HALF]]
    all_to_all x3 -> x0, local copies, waits for them, and re-layouts: 21.7 us -> none  [the longest x2 19.2 us: per_device(): lax.all_to_all(whole_cycles, 'pts', split_axis=2, concat_axis=0, tiled=True)]
  transfers between devices with their start and end apart: 4 -> 2, of which waited for: 4 -> 2; matrix products, arithmetic and copies ran while one was open for 2% -> 1% of each run, Pallas kernels for 0% -> 0%
where the time goes in v1:
time: 203 us; the launch traced here: 202 us
  blocking collectives  70.6 us (35%)
  waiting for transfers between devices  57.1 us (28%)
  Pallas kernels  52.3 us (26%)
  starting transfers between devices  15.6 us (8%)
  local copies, waits for them, and re-layouts  5.79 us (3%)
    all_to_all x1, blocking collectives, per_device(): lax.all_to_all(picked, ('pts', 'tile'), split_axis=0, concat_axis=0, tile...  35.7 us
    all_to_all x1, blocking collectives, per_device(): lax.all_to_all(whole, 'pts', split_axis=0, concat_axis=0, tiled=True)  34.9 us
    all_to_all x1, waiting for transfers between devices, per_device(): lax.all_to_all(partial, ('pts', 'tile'), split_axis=0, concat_axis=0, til...  29.9 us
    all_to_all x1, waiting for transfers between devices, per_device(): lax.all_to_all(owned, 'pts', split_axis=0, concat_axis=0, tiled=True)  27.2 us
    pallas_call x1, Pallas kernels, spread(): pl.pallas_call(spread_kernel, grid=(slots // block,), in_specs=[flat, tap...  21.5 us
    pallas_call x1, Pallas kernels, read_back(): pl.pallas_call(read_kernel, grid=(slots // block,), in_specs=[pl.BlockSpe...  12.5 us
    all_to_all x1, starting transfers between devices, per_device(): lax.all_to_all(partial, ('pts', 'tile'), split_axis=0, concat_axis=0, til...  11.5 us
    pallas_call x1, Pallas kernels, filter_cycles(): pl.pallas_call(filter_kernel, grid=(count // block,), in_specs=[spec, who...  11 us
  transfers between devices with their start and end apart: 2, of which 2 were waited for; matrix products, arithmetic and copies ran while one was open for 1% of the time, Pallas kernels for 0%

profile of v1, /device:TPU:1, one launch (start us, length us, event | category | flops | bytes accessed | tf_op | source)
XLA Modules:
  0.0 202.2 jit_solution(6796289091719841981)
XLA Ops:
  0.6 0.0 copy-start
  0.6 21.5 %spread.1 = f32[32,4,2,8,256]{4,3,2,1,0:T(8,128)} custom-call(f32[64,1024]{1,0:T(8,128)} %bitcast.31, f32[64,8,1024]{2,1,0:T(8,128)} %bitcast.18, f32[64,8,1024]{2,1,0:T(8,128)} %bitcast.20, s32[64,1024]{1,0:T(8,128)} %bitcast.27, s32[64,1024]{1,0:T(8,128)} %bitcast.29), custom_call_target="tpu_custom_call" | custom-call | tf_op jit(solution)/shard_map/spread/pallas_call | solution.py:71
  22.2 11.5 %all-to-all-start = ((f32[128,2,8,256]{3,2,1,0:T(8,128)}), f32[128,2,8,256]{3,2,1,0:T(8,128)S(1)}, u32[]{:S(2)}, u32[]{:S(2)}) async-start(f32[128,2,8,256]{3,2,1,0:T(8,128)} %bitcast.22), calls=%async_computation | async-start | bytes 4194304 | tf_op jit(solution)/shard_map/all_to_all | solution.py:277
  33.7 0.0 copy-done
  33.7 0.1 copy.12
  33.8 0.7 reshape.30.j_ref
  34.5 29.9 %all-to-all-done = f32[128,2,8,256]{3,2,1,0:T(8,128)S(1)} async-done(((f32[128,2,8,256]{3,2,1,0:T(8,128)}), f32[128,2,8,256]{3,2,1,0:T(8,128)S(1)}, u32[]{:S(2)}, u32[]{:S(2)}) %all-to-all-start) | async-done | bytes 2097184 | tf_op jit(solution)/shard_map/all_to_all | solution.py:277
  64.4 0.0 copy-start.2
  64.4 1.3 copy-done.2
  65.8 3.8 %accumulate.1 = f32[256,8,256]{2,1,0:T(8,128)} custom-call(s32[256]{0:T(256)} %reshape.30.j_ref, f32[256,8,256]{2,1,0:T(8,128)} %bitcast.24), custom_call_target="tpu_custom_call" | custom-call | tf_op jit(solution)/shard_map/accumulate/pallas_call | solution.py:139
  69.6 0.0 copy-start.4
  69.6 4.1 %all-to-all-start.1 = ((f32[256,8,256]{2,1,0:T(8,128)}), f32[256,8,256]{2,1,0:T(8,128)S(1)}, u32[]{:S(2)}, u32[]{:S(2)}) async-start(f32[256,8,256]{2,1,0:T(8,128)} %accumulate.1), calls=%async_computation.1 | async-start | bytes 4194304 | tf_op jit(solution)/shard_map/all_to_all | solution.py:280
  73.7 0.0 copy-done.4
  73.8 0.1 slice.6
  73.8 0.1 reverse
  73.9 0.1 slice.9
  74.0 0.1 maximum_multiply_fusion
  74.1 0.1 mul.12
  74.2 0.1 copy.13
  74.2 0.6 slice.8.gain_ref
  74.9 27.2 %all-to-all-done.1 = f32[256,8,256]{2,1,0:T(8,128)S(1)} async-done(((f32[256,8,256]{2,1,0:T(8,128)}), f32[256,8,256]{2,1,0:T(8,128)S(1)}, u32[]{:S(2)}, u32[]{:S(2)}) %all-to-all-start.1) | async-done | bytes 2097184 | tf_op jit(solution)/shard_map/all_to_all | solution.py:280
  102.1 0.0 copy-start.3
  102.1 1.3 copy-done.3
  103.4 11.0 %filter.1 = f32[32,64,256]{2,1,0:T(8,128)} custom-call(f32[32,64,256]{2,1,0:T(8,128)} %bitcast.25, f32[17,256]{1,0:T(8,128)} %slice.8.gain_ref, f32[2,17,256]{2,1,0:T(8,128)} %constant.20.clone.twist_ref, bf16[256,512]{1,0:T(8,128)(2,1)} %constant.21.clone.high_ref, bf16[256,512]{1,0:T(8,128)(2,1)} %constant.22.clone.low_ref), custom_call_target="tpu_custom_call" | custom-call | tf_op jit(solution)/shard_map/filter/pallas_call | solution.py:262
  114.4 34.9 %all_to_all.20 = f32[32,64,256]{2,1,0:T(8,128)} all-to-all(f32[32,64,256]{2,1,0:T(8,128)} %filter.1), channel_id=1, replica_groups=mesh['pts'=32,'tile'=4] {'pts'}, dimensions={0} | all-to-all | bytes 4194304 | tf_op jit(solution)/shard_map/all_to_all | solution.py:282
  149.3 3.4 %pick.1 = f32[256,8,256]{2,1,0:T(8,128)} custom-call(s32[256]{0:T(256)} %reshape.30.j_ref, f32[256,8,256]{2,1,0:T(8,128)} %bitcast.16), custom_call_target="tpu_custom_call" | custom-call | tf_op jit(solution)/shard_map/pick/pallas_call | solution.py:139
  152.7 35.7 %all_to_all.21 = f32[128,2,8,256]{3,2,1,0:T(8,128)} all-to-all(f32[128,2,8,256]{3,2,1,0:T(8,128)} %bitcast.26), channel_id=1, replica_groups=mesh['pts'=32,'tile'=4] {'pts','tile'}, dimensions={0} | all-to-all | bytes 4194304 | tf_op jit(solution)/shard_map/all_to_all | solution.py:286
  188.3 0.0 copy-start.1
  188.3 12.5 %read_back.1 = f32[64,1024]{1,0:T(8,128)} custom-call(f32[32,4,2,8,256]{4,3,2,1,0:T(8,128)} %bitcast.23, f32[64,8,1024]{2,1,0:T(8,128)} %bitcast.19, f32[64,8,1024]{2,1,0:T(8,128)} %bitcast.21, s32[64,1024]{1,0:T(8,128)} %bitcast.28, s32[64,1024]{1,0:T(8,128)} %bitcast.30), custom_call_target="tpu_custom_call" | custom-call | tf_op jit(solution)/shard_map/read_back/pallas_call | solution.py:102
  200.9 0.0 copy-done.1
  200.9 1.3 copy.15
  (1 shorter events, 0.0 us)
Async XLA Ops:
  0.6 33.1 %copy-start = (s32[128,32,2]{0,2,1:T(2,128)S(1)}, s32[128,32,2]{0,2,1:T(2,128)}, u32[]{:S(2)}) copy-start(s32[128,32,2]{0,2,1:T(2,128)} %param.15) | copy-start | bytes 98308
  22.2 42.2 %all-to-all-start = ((f32[128,2,8,256]{3,2,1,0:T(8,128)}), f32[128,2,8,256]{3,2,1,0:T(8,128)S(1)}, u32[]{:S(2)}, u32[]{:S(2)}) async-start(f32[128,2,8,256]{3,2,1,0:T(8,128)} %bitcast.22), calls=%async_computation | async-start | bytes 4194304 | tf_op jit(solution)/shard_map/all_to_all | solution.py:277
  64.4 1.3 copy-start.2
  69.6 4.2 %copy-start.4 = (f32[4097]{0:T(1024)S(1)}, f32[4097]{0:T(1024)}, u32[]{:S(2)}) copy-start(f32[4097]{0:T(1024)} %param.16) | copy-start | bytes 49168
  69.6 32.5 %all-to-all-start.1 = ((f32[256,8,256]{2,1,0:T(8,128)}), f32[256,8,256]{2,1,0:T(8,128)S(1)}, u32[]{:S(2)}, u32[]{:S(2)}) async-start(f32[256,8,256]{2,1,0:T(8,128)} %accumulate.1), calls=%async_computation.1 | async-start | bytes 4194304 | tf_op jit(solution)/shard_map/all_to_all | solution.py:280
  102.1 1.3 copy-start.3
  188.3 12.5 %copy-start.1 = (f32[32,64,256]{2,1,0:T(8,128)S(1)}, f32[32,64,256]{2,1,0:T(8,128)}, u32[]{:S(2)}) copy-start(f32[32,64,256]{2,1,0:T(8,128)} %all_to_all.20) | copy-start | bytes 6291460

commit v2 on v1

--- a/solution.py
+++ b/solution.py
@@ -51,68 +51,151 @@
     return [jnp.concatenate(out, 0) for out in rows]
 
 
-def spread_kernel(v_ref, ct_ref, pt_ref, cs_ref, ps_ref, o_ref):
-    for s in range(v_ref.shape[0]):
-        cycle, cycle_group = place(ct_ref[s] * v_ref[s : s + 1, :], cs_ref[s : s + 1, :])
-        phi, phi_group = place(pt_ref[s], ps_ref[s : s + 1, :])
-        cycle_high, cycle_low = expand(split(cycle), cycle_group, TR // 8)
-        phi_high, phi_low = expand(split(phi), phi_group, TP // 8)
-        stacked = jnp.concatenate([cycle_high, cycle_low], 0)
-        first = lax.dot_general(phi_high, stacked, CONTRACT_LAST, preferred_element_type=F32)
-        second = lax.dot_general(phi_low, cycle_high, CONTRACT_LAST, preferred_element_type=F32)
-        tile = (first[:, :TR] + first[:, TR:] + second).T
-        o_ref[s // 2, :, s % 2] = tile.reshape(4, 8, TP)
-
-
-def spread(values, cycle_taps, phi_taps, cycle_start, phi_start, block=8):
-    slots = values.shape[0]
-    flat = pl.BlockSpec((block, PPS), lambda i: (i, 0))
-    taps = pl.BlockSpec((block, 8, PPS), lambda i: (i, 0, 0))
+MESH = pl.DeviceIdType.MESH
+TILES = 4
+
+
+def spread_tile(values, cycle_taps, phi_taps, cycle_start, phi_start):
+    cycle, cycle_group = place(cycle_taps * values, cycle_start)
+    phi, phi_group = place(phi_taps, phi_start)
+    cycle_high, cycle_low = expand(split(cycle), cycle_group, TR // 8)
+    phi_high, phi_low = expand(split(phi), phi_group, TP // 8)
+    stacked = jnp.concatenate([cycle_high, cycle_low], 0)
+    first = lax.dot_general(phi_high, stacked, CONTRACT_LAST, preferred_element_type=F32)
+    second = lax.dot_general(phi_low, cycle_high, CONTRACT_LAST, preferred_element_type=F32)
+    return (first[:, :TR] + first[:, TR:] + second).T
+
+
+def read_tile(tile, cycle_taps, phi_taps, cycle_start, phi_start):
+    tile_high, tile_low = split(tile)
+    cycle, cycle_group = place(cycle_taps, cycle_start)
+    phi, phi_group = place(phi_taps, phi_start)
+    cycle_high, cycle_low = expand(split(cycle), cycle_group, TR // 8)
+    right = jnp.concatenate([cycle_high, cycle_low, cycle_high], 0)
+    left = jnp.concatenate([tile_high, tile_high, tile_low], 0).T
+    along = jnp.dot(left, right, preferred_element_type=F32)
+    picked = jnp.zeros((8, PPS), F32)
+    for g in range(TP // 8):
+        picked = jnp.where(phi_group == g, along[8 * g : 8 * g + 8], picked)
+    return jnp.sum(picked * phi, 0, keepdims=True)
+
+
+class Place:
+    def __init__(self):
+        self.column = lax.axis_index("pts")
+        self.part = lax.axis_index("tile")
+        self.z = self.column // 8
+        self.y = lax.rem(self.column // 2, 4)
+        self.core = lax.rem(self.column, 2)
+
+    def offsets(self, i):
+        far = lambda k: lax.rem(2 + 3 * k + 3 * (k * (k - 1) // 2), 4)
+        a, b = lax.rem(i, 4), lax.rem(i // 4, 4)
+        return far(a), far(lax.rem(a + b, 4)), 1 - i // 16
+
+    def target(self, i):
+        dz, dy, dc = self.offsets(i)
+        z, y = lax.rem(self.z + dz, 4), lax.rem(self.y + dy, 4)
+        return (z * 4 + y) * 2 + lax.rem(self.core + dc, 2)
+
+    def source(self, i):
+        dz, dy, dc = self.offsets(i)
+        z, y = lax.rem(self.z + 4 - dz, 4), lax.rem(self.y + 4 - dy, 4)
+        return (z * 4 + y) * 2 + lax.rem(self.core + dc, 2)
+
+    def parts(self, i):
+        return [lax.rem(self.part + lax.rem(i, 4) + step, 4) for step in range(TILES)]
+
+    def other(self, column, part):
+        return jnp.logical_or(column != self.column, part != self.part)
+
+
+def greet(here):
+    barrier = pltpu.get_barrier_semaphore()
+
+    def step(i, carry):
+        column = here.target(i)
+        for part in here.parts(i):
+
+            @pl.when(here.other(column, part))
+            def _():
+                pl.semaphore_signal(
+                    barrier, inc=1, device_id=(column, part), device_id_type=MESH
+                )
+
+        return carry
+
+    lax.fori_loop(0, COLS, step, 0)
+    return barrier
+
+
+def bytes_of(ref, sem):
+    return pltpu.make_async_copy(ref, ref, sem)
+
+
+def spread_kernel(v_ref, ct_ref, pt_ref, cs_ref, ps_ref, o_ref, stage, send, recv, local):
+    here = Place()
+    barrier = greet(here)
+    me = here.column * TILES + here.part
+
+    def compute(step):
+        for half in range(2):
+            column = here.target(2 * step + half)
+            for k in range(2):
+                slot = 2 * column + k
+                row = pl.ds(slot, 1)
+                tile = spread_tile(
+                    v_ref[row, :], ct_ref[slot], pt_ref[slot], cs_ref[row, :], ps_ref[row, :]
+                )
+                stage[pl.ds(column * TILES, TILES), k] = tile.reshape(TILES, 8, TP)
+
+    def dispatch(step):
+        for half in range(2):
+            i = 2 * step + half
+            column = here.target(i)
+            for part in here.parts(i):
+
+                @pl.when(here.other(column, part))
+                def _():
+                    pltpu.make_async_remote_copy(
+                        stage.at[column * TILES + part],
+                        o_ref.at[me],
+                        send,
+                        recv,
+                        device_id=(column, part),
+                        device_id_type=MESH,
+                    ).start()
+
+    compute(0)
+    pl.semaphore_wait(barrier, COLS * TILES - 1)
+
+    def step(i, carry):
+        compute(i)
+        dispatch(i - 1)
+        return carry
+
+    lax.fori_loop(1, COLS // 2, step, 0)
+    dispatch(COLS // 2 - 1)
+    own = pltpu.make_async_copy(stage.at[me], o_ref.at[me], local)
+    own.start()
+    own.wait()
+    others = pl.ds(0, COLS * TILES - 1)
+    bytes_of(stage.at[others], send).wait()
+    bytes_of(o_ref.at[others], recv).wait()
+
+
+def spread(values, cycle_taps, phi_taps, cycle_start, phi_start):
+    vmem = pl.BlockSpec(memory_space=pltpu.VMEM)
+    shape = (COLS * TILES, 2, 8, TP)
     return pl.pallas_call(
         spread_kernel,
-        grid=(slots // block,),
-        in_specs=[flat, taps, taps, flat, flat],
-        out_specs=pl.BlockSpec((block // 2, 4, 2, 8, TP), lambda i: (i, 0, 0, 0, 0)),
-        out_shape=jax.ShapeDtypeStruct((slots // 2, 4, 2, 8, TP), F32),
+        in_specs=[vmem] * 5,
+        out_specs=pl.BlockSpec(memory_space=pl.ANY),
+        out_shape=jax.ShapeDtypeStruct(shape, F32),
+        scratch_shapes=[pltpu.VMEM(shape, F32)] + [pltpu.SemaphoreType.DMA] * 3,
+        compiler_params=pltpu.CompilerParams(collective_id=0, has_side_effects=True),
         name="spread",
     )(values, cycle_taps, phi_taps, cycle_start, phi_start)
-
-
-def read_kernel(f_ref, ct_ref, pt_ref, cs_ref, ps_ref, o_ref):
-    rows = []
-    for s in range(ct_ref.shape[0]):
-        tile_high, tile_low = split(f_ref[s // 2, :, s % 2].reshape(TR, TP))
-        cycle, cycle_group = place(ct_ref[s], cs_ref[s : s + 1, :])
-        phi, phi_group = place(pt_ref[s], ps_ref[s : s + 1, :])
-        cycle_high, cycle_low = expand(split(cycle), cycle_group, TR // 8)
-        right = jnp.concatenate([cycle_high, cycle_low, cycle_high], 0)
-        left = jnp.concatenate([tile_high, tile_high, tile_low], 0).T
-        along = jnp.dot(left, right, preferred_element_type=F32)
-        picked = jnp.zeros((8, PPS), F32)
-        for g in range(TP // 8):
-            picked = jnp.where(phi_group == g, along[8 * g : 8 * g + 8], picked)
-        rows.append(jnp.sum(picked * phi, 0, keepdims=True))
-    o_ref[...] = jnp.concatenate(rows, 0)
-
-
-def read_back(tiles, cycle_taps, phi_taps, cycle_start, phi_start, block=8):
-    slots = cycle_taps.shape[0]
-    flat = pl.BlockSpec((block, PPS), lambda i: (i, 0))
-    taps = pl.BlockSpec((block, 8, PPS), lambda i: (i, 0, 0))
-    return pl.pallas_call(
-        read_kernel,
-        grid=(slots // block,),
-        in_specs=[
-            pl.BlockSpec((block // 2, 4, 2, 8, TP), lambda i: (i, 0, 0, 0, 0)),
-            taps,
-            taps,
-            flat,
-            flat,
-        ],
-        out_specs=flat,
-        out_shape=jax.ShapeDtypeStruct((slots, PPS), F32),
-        name="read_back",
-    )(tiles, cycle_taps, phi_taps, cycle_start, phi_start)
 
 
 def accumulate_kernel(j_ref, a_ref, o_ref):
@@ -124,14 +207,6 @@
         return carry
 
     lax.fori_loop(0, a_ref.shape[0], step, 0, unroll=8)
-
-
-def pick_kernel(j_ref, f_ref, o_ref):
-    def step(i, carry):
-        o_ref[i] = f_ref[j_ref[i]]
-        return carry
-
-    lax.fori_loop(0, o_ref.shape[0], step, 0, unroll=8)
 
 
 def by_index(kernel, name, index, tiles, count):
@@ -206,9 +281,9 @@
     return dot(high, table_high) + dot(high, table_low) + dot(low, table_high)
 
 
-def filter_kernel(x_ref, gain_ref, twist_ref, high_ref, low_ref, o_ref):
-    cycles = x_ref.shape[1]
-    spec = real_fft([x_ref[q] for q in range(COLS)])
+def filter_rows(rows, gain_ref, twist_ref, high_ref, low_ref):
+    cycles = rows[0].shape[0]
+    spec = real_fft(rows)
     reals, imags = [], []
     for k in range(HALF):
         cos, sin = twist_ref[0, k : k + 1, :], twist_ref[1, k : k + 1, :]
@@ -238,8 +313,7 @@
         cos, sin = twist_ref[0, k : k + 1, :], twist_ref[1, k : k + 1, :]
         re, im = back_re[k * cycles : (k + 1) * cycles], back_im[k * cycles : (k + 1) * cycles]
         spec.append(times(re, im, cos, sin))
-    for q, row in enumerate(real_inverse(spec)):
-        o_ref[q] = row
+    return real_inverse(spec)
 
 
 def filter_tables():
@@ -252,39 +326,221 @@
     return np.stack([np.cos(angle), np.sin(angle)]).astype(np.float32), high, low
 
 
-def filter_cycles(cycles, response, block=16):
-    count = cycles.shape[1]
+CHUNKS = 4
+CHUNK_J = 2
+
+
+def filter_kernel(
+    j_ref, owned_ref, gain_ref, twist_ref, high_ref, low_ref, ct_hbm, pt_hbm, cs_hbm, ps_hbm,
+    filtered_ref, gradient_ref,
+    ct_ref, pt_ref, cs_ref, ps_ref, arrived, ready, filtered, picked, returned,
+    load_sem, out_sem, send_in, recv_in, own_in, send_out, recv_out, own_out,
+    send_pick, recv_pick, own_pick,
+):
+    here = Place()
+    barrier = greet(here)
+    me, mine = here.column, here.part
+    loads = [
+        pltpu.make_async_copy(source, target, load_sem.at[n])
+        for n, (source, target) in enumerate(
+            [(ct_hbm, ct_ref), (pt_hbm, pt_ref), (cs_hbm, cs_ref), (ps_hbm, ps_ref)]
+        )
+    ]
+
+    def rows_of(column, chunk):
+        return pl.ds(column * (CHUNKS * CHUNK_J) + chunk * CHUNK_J, CHUNK_J)
+
+    def own_row(chunk):
+        return pltpu.make_async_copy(
+            owned_ref.at[rows_of(me, chunk)], arrived.at[chunk, me], own_in.at[chunk]
+        )
+
+    for chunk in range(CHUNKS):
+        own_row(chunk).start()
+    pl.semaphore_wait(barrier, COLS * TILES - 1)
+
+    def send_rows(n, carry):
+        chunk, i = n // COLS, lax.rem(n, COLS)
+        column = here.target(i)
+
+        @pl.when(column != me)
+        def _():
+            pltpu.make_async_remote_copy(
+                owned_ref.at[rows_of(column, chunk)],
+                arrived.at[chunk, me],
+                send_in,
+                recv_in.at[chunk],
+                device_id=(column, mine),
+                device_id_type=MESH,
+            ).start()
+
+        return carry
+
+    lax.fori_loop(0, CHUNKS * COLS, send_rows, 0)
+    for load in loads:
+        load.start()
+
+    def filter_chunk(chunk, carry):
+        bytes_of(arrived.at[chunk, pl.ds(0, COLS - 1)], recv_in.at[chunk]).wait()
+        own_row(chunk).wait()
+        rows = [arrived[chunk, q].reshape(CHUNK_J * 8, TP) for q in range(COLS)]
+        rows = filter_rows(rows, gain_ref, twist_ref, high_ref, low_ref)
+        for q in range(COLS):
+            ready[chunk, q] = rows[q].reshape(CHUNK_J, 8, TP)
+
+        def send_ready(i, carry):
+            column = here.target(i)
+
+            @pl.when(column != me)
+            def _():
+                pltpu.make_async_remote_copy(
+                    ready.at[chunk, column],
+                    filtered.at[rows_of(me, chunk)],
+                    send_out,
+                    recv_out,
+                    device_id=(column, mine),
+                    device_id_type=MESH,
+                ).start()
+
+            return carry
+
+        lax.fori_loop(0, COLS, send_ready, 0)
+        pltpu.make_async_copy(
+            ready.at[chunk, me], filtered.at[rows_of(me, chunk)], own_out.at[chunk]
+        ).start()
+        return carry
+
+    lax.fori_loop(0, CHUNKS, filter_chunk, 0)
+    for chunk in range(CHUNKS):
+        pltpu.make_async_copy(
+            ready.at[chunk, me], filtered.at[rows_of(me, chunk)], own_out.at[chunk]
+        ).wait()
+    bytes_of(filtered.at[pl.ds(0, NJ - CHUNKS * CHUNK_J)], recv_out).wait()
+    store = pltpu.make_async_copy(filtered, filtered_ref, out_sem)
+    store.start()
+
+    def pick_and_send(i, carry):
+        column = here.target(i)
+        for part in range(TILES):
+            block = column * TILES + part
+            for k in range(2):
+                picked[block, k] = filtered[j_ref[2 * block + k]]
+        for part in here.parts(i):
+
+            @pl.when(here.other(column, part))
+            def _():
+                pltpu.make_async_remote_copy(
+                    picked.at[column * TILES + part],
+                    returned.at[me, mine],
+                    send_pick,
+                    recv_pick.at[me],
+                    device_id=(column, part),
+                    device_id_type=MESH,
+                ).start()
+
+        return carry
+
+    lax.fori_loop(0, COLS, pick_and_send, 0)
+    own = pltpu.make_async_copy(picked.at[me * TILES + mine], returned.at[me, mine], own_pick)
+    own.start()
+    for load in loads:
+        load.wait()
+    own.wait()
+
+    def read(i, carry):
+        column = here.source(i)
+
+        @pl.when(column != me)
+        def _():
+            bytes_of(returned.at[column], recv_pick.at[column]).wait()
+
+        @pl.when(column == me)
+        def _():
+            bytes_of(returned.at[column, pl.ds(0, TILES - 1)], recv_pick.at[column]).wait()
+
+        for k in range(2):
+            slot = 2 * column + k
+            row = pl.ds(slot, 1)
+            gradient_ref[row, :] = read_tile(
+                returned[column, :, k].reshape(TR, TP),
+                ct_ref[slot],
+                pt_ref[slot],
+                cs_ref[row, :],
+                ps_ref[row, :],
+            )
+        return carry
+
+    lax.fori_loop(0, COLS, read, 0)
+    bytes_of(arrived.at[:, pl.ds(0, COLS - 1)], send_in).wait()
+    bytes_of(ready.at[:, pl.ds(0, COLS - 1)], send_out).wait()
+    bytes_of(picked.at[pl.ds(0, COLS * TILES - 1)], send_pick).wait()
+    store.wait()
+
+
+def filter_and_read(wanted, owned, response, cycle_taps, phi_taps, cycle_start, phi_start):
     full = jnp.concatenate([response, response[-2:0:-1]]) * (1.0 / NPHI)
     gain = full.reshape(TP, COLS).T[:HALF]
     twist, high, low = filter_tables()
-    spec = pl.BlockSpec((COLS, block, TP), lambda i: (0, i, 0))
-    whole = lambda *shape: pl.BlockSpec(shape, lambda i: (0,) * len(shape))
+    vmem = pl.BlockSpec(memory_space=pltpu.VMEM)
+    hbm = pl.BlockSpec(memory_space=pl.ANY)
+    tiles = (COLS * TILES, 2, 8, TP)
+    blocks = (CHUNKS, COLS, CHUNK_J, 8, TP)
+    dma = pltpu.SemaphoreType.DMA
     return pl.pallas_call(
         filter_kernel,
-        grid=(count // block,),
-        in_specs=[spec, whole(HALF, TP), whole(2, HALF, TP), whole(TP, 2 * TP), whole(TP, 2 * TP)],
-        out_specs=spec,
-        out_shape=jax.ShapeDtypeStruct(cycles.shape, F32),
-        name="filter",
-    )(cycles, gain, jnp.asarray(twist), jnp.asarray(high), jnp.asarray(low))
+        in_specs=[pl.BlockSpec(memory_space=pltpu.SMEM), hbm] + [vmem] * 4 + [hbm] * 4,
+        out_specs=(hbm, vmem),
+        out_shape=(
+            jax.ShapeDtypeStruct((NJ, 8, TP), F32),
+            jax.ShapeDtypeStruct((SLOTS_DEV, PPS), F32),
+        ),
+        scratch_shapes=[
+            pltpu.VMEM(cycle_taps.shape, F32),
+            pltpu.VMEM(phi_taps.shape, F32),
+            pltpu.VMEM(cycle_start.shape, jnp.int32),
+            pltpu.VMEM(phi_start.shape, jnp.int32),
+            pltpu.VMEM(blocks, F32),
+            pltpu.VMEM(blocks, F32),
+            pltpu.VMEM((NJ, 8, TP), F32),
+            pltpu.VMEM(tiles, F32),
+            pltpu.VMEM((COLS, TILES, 2, 8, TP), F32),
+            dma((4,)),
+            dma,
+            dma,
+            dma((CHUNKS,)),
+            dma((CHUNKS,)),
+            dma,
+            dma,
+            dma((CHUNKS,)),
+            dma,
+            dma((COLS,)),
+            dma,
+        ],
+        compiler_params=pltpu.CompilerParams(
+            collective_id=1, has_side_effects=True, vmem_limit_bytes=48 << 20
+        ),
+        name="filter_and_read",
+    )(
+        wanted,
+        owned,
+        gain,
+        jnp.asarray(twist),
+        jnp.asarray(high),
+        jnp.asarray(low),
+        cycle_taps,
+        phi_taps,
+        cycle_start,
+        phi_start,
+    )
 
 
 def per_device(values, cycle_taps, phi_taps, cycle_start, phi_start, tile_list, response):
+    points = (cycle_taps[0], phi_taps[0], cycle_start[0], phi_start[0])
+    arrived = spread(values[0], *points)
     column = lax.axis_index("pts")
-    part_count = lax.axis_size("tile")
-    points = (cycle_taps[0], phi_taps[0], cycle_start[0], phi_start[0])
-    partial = spread(values[0], *points).reshape(COLS * part_count, 2, 8, TP)
-    arrived = lax.all_to_all(partial, ("pts", "tile"), split_axis=0, concat_axis=0, tiled=True)
     wanted = lax.dynamic_index_in_dim(tile_list, column, 1, keepdims=False).reshape(-1)
     owned = by_index(accumulate_kernel, "accumulate", wanted, arrived.reshape(-1, 8, TP), NJ)
-    cycles = lax.all_to_all(owned, "pts", split_axis=0, concat_axis=0, tiled=True)
-    whole = filter_cycles(cycles.reshape(COLS, -1, TP), response)
-    filtered = lax.all_to_all(whole, "pts", split_axis=0, concat_axis=0, tiled=True)
-    filtered = filtered.reshape(NJ, 8, TP)
-    picked = by_index(pick_kernel, "pick", wanted, filtered, wanted.size)
-    picked = picked.reshape(COLS * part_count, 2, 8, TP)
-    returned = lax.all_to_all(picked, ("pts", "tile"), split_axis=0, concat_axis=0, tiled=True)
-    gradient = read_back(returned.reshape(COLS, part_count, 2, 8, TP), *points)
+    filtered, gradient = filter_and_read(wanted, owned, response, *points)
     return filtered, gradient[None]
 
 

time: 203 us -> 145 us (0.71)
  Pallas kernels: 52.3 us -> 136 us
  blocking collectives: 70.6 us -> 0 us
  waiting for transfers between devices: 57.1 us -> 0 us
  starting transfers between devices: 15.6 us -> 0 us
    pallas_call x3 -> x2, Pallas kernels: 45.1 us -> 132 us  [the longest x1 89.6 us: filter_and_read(): pl.pallas_call(filter_kernel, in_specs=[pl.BlockSpec(memory_space=pltpu.S...]
    all_to_all x2 -> x0, blocking collectives: 70.6 us -> none  [the longest x1 35.7 us: per_device(): lax.all_to_all(picked, ('pts', 'tile'), split_axis=0, concat_axis=0, tile...]
    all_to_all x2 -> x0, waiting for transfers between devices: 57.1 us -> none  [the longest x1 29.9 us: per_device(): lax.all_to_all(partial, ('pts', 'tile'), split_axis=0, concat_axis=0, til...]
    all_to_all x2 -> x0, starting transfers between devices: 15.6 us -> none  [the longest x1 11.5 us: per_device(): lax.all_to_all(partial, ('pts', 'tile'), split_axis=0, concat_axis=0, til...]
    pallas_call x2 -> x1, Pallas kernels: 7.19 us -> 3.89 us  [by_index(): pl.pallas_call(kernel, in_specs=[pl.BlockSpec(memory_space=pltpu.SMEM), v...]
    unnamed x13 -> x20, local copies, waits for them, and re-layouts: 4.13 us -> 4.56 us
  transfers between devices with their start and end apart: 2 -> 0, of which waited for: 2 -> 0; matrix products, arithmetic and copies ran while one was open for 1% -> 0% of each run, Pallas kernels for 0% -> 0%
where the time goes in v2:
time: 145 us; the launch traced here: 144 us
  Pallas kernels  136 us (94%)
  local copies, waits for them, and re-layouts  6.33 us (4%)
    pallas_call x1, Pallas kernels, filter_and_read(): pl.pallas_call(filter_kernel, in_specs=[pl.BlockSpec(memory_space=pltpu.S...  89.6 us
    pallas_call x1, Pallas kernels, spread(): pl.pallas_call(spread_kernel, in_specs=[vmem] * 5, out_specs=pl.BlockSpec...  42.1 us
    unnamed x20, local copies, waits for them, and re-layouts  4.56 us
    pallas_call x1, Pallas kernels, by_index(): pl.pallas_call(kernel, in_specs=[pl.BlockSpec(memory_space=pltpu.SMEM), v...  3.89 us

profile of v2, /device:TPU:1, one launch (start us, length us, event | category | flops | bytes accessed | tf_op | source)
XLA Modules:
  0.0 143.5 jit_solution(623279588334334745)
XLA Ops:
  0.6 0.0 copy-start
  0.6 0.7 copy-done
  1.4 0.8 slice.6
  2.2 0.1 reverse
  2.3 0.1 slice.9
  2.4 0.8 maximum_multiply_fusion
  3.2 0.1 copy.12
  3.3 0.7 reshape.15.j_ref
  4.0 0.1 mul.12
  4.1 0.1 copy.13
  4.1 42.1 %spread.1 = f32[128,2,8,256]{3,2,1,0:T(8,128)} custom-call(f32[64,1024]{1,0:T(8,128)} %bitcast.21, f32[64,8,1024]{2,1,0:T(8,128)} %bitcast.16, f32[64,8,1024]{2,1,0:T(8,128)} %bitcast.18, s32[64,1024]{1,0:T(8,128)} %bitcast.11, s32[64,1024]{1,0:T(8,128)} %bitcast.13), custom_call_target="tpu_custom_call" | custom-call | tf_op jit(solution)/shard_map/spread/pallas_call | solution.py:190
  46.3 0.0 copy-start.2
  46.3 0.0 copy-start.3
  46.3 0.0 copy-start.4
  46.3 0.0 copy-start.5
  46.3 0.0 copy-start.6
  46.3 0.0 copy-start.7
  46.3 3.9 %accumulate.1.owned_ref = f32[256,8,256]{2,1,0:T(8,128)} custom-call(s32[256]{0:T(256)} %reshape.15.j_ref, f32[256,8,256]{2,1,0:T(8,128)} %bitcast.20), custom_call_target="tpu_custom_call" | custom-call | tf_op jit(solution)/shard_map/accumulate/pallas_call | solution.py:214
  50.2 0.0 copy-done.2
  50.2 0.0 copy-done.3
  50.2 0.0 copy-done.4
  50.2 0.0 copy-done.5
  50.3 0.0 copy-done.6
  50.3 0.0 copy-done.7
  50.3 0.0 copy-start.1
  50.3 1.6 %copy-done.1 = f32[256,8,256]{2,1,0:T(8,128)S(1)} copy-done((f32[256,8,256]{2,1,0:T(8,128)S(1)}, f32[256,8,256]{2,1,0:T(8,128)}, u32[]{:S(2)}) %copy-start.1) | copy-done | bytes 2097176
  51.9 89.6 %filter_and_read.1 = (f32[256,8,256]{2,1,0:T(8,128)S(1)}, f32[64,1024]{1,0:T(8,128)S(1)}) custom-call(s32[256]{0:T(256)S(1)} %copy-done.7, f32[256,8,256]{2,1,0:T(8,128)S(1)} %copy-done.1, f32[17,256]{1,0:T(8,128)S(1)} %slice.8.gain_ref, f32[2,17,256]{2,1,0:T(8,128)S(1)} %copy-done.6, bf16[256,512]{1,0:T(8,128)(2,1)S(1)} %copy-done.5, ...), custom_call_target="tpu_custom_call" | custom-call | tf_op jit(solution)/shard_map/filter_and_read/pallas_call | solution.py:489
  141.5 1.3 copy.16
  142.8 0.7 copy.17
  (2 shorter events, 0.0 us)
Async XLA Ops:
  0.6 0.8 copy-start
  46.3 4.0 %copy-start.2 = (s32[1,64,1024]{2,1,0:T(8,128)S(1)}, s32[1,64,1024]{2,1,0:T(8,128)}, u32[]{:S(2)}) copy-start(s32[1,64,1024]{2,1,0:T(8,128)} %param.13) | copy-start | bytes 786436
  46.3 4.0 %copy-start.3 = (s32[1,64,1024]{2,1,0:T(8,128)S(1)}, s32[1,64,1024]{2,1,0:T(8,128)}, u32[]{:S(2)}) copy-start(s32[1,64,1024]{2,1,0:T(8,128)} %param.14) | copy-start | bytes 786436
  46.3 3.9 %copy-start.4 = (bf16[256,512]{1,0:T(8,128)(2,1)S(1)}, bf16[256,512]{1,0:T(8,128)(2,1)}, u32[]{:S(2)}) copy-start(bf16[256,512]{1,0:T(8,128)(2,1)} %constant.22.clone.low_ref) | copy-start | bytes 786436
  46.3 3.9 %copy-start.5 = (bf16[256,512]{1,0:T(8,128)(2,1)S(1)}, bf16[256,512]{1,0:T(8,128)(2,1)}, u32[]{:S(2)}) copy-start(bf16[256,512]{1,0:T(8,128)(2,1)} %constant.21.clone.high_ref) | copy-start | bytes 786436
  46.3 3.9 %copy-start.6 = (f32[2,17,256]{2,1,0:T(8,128)S(1)}, f32[2,17,256]{2,1,0:T(8,128)}, u32[]{:S(2)}) copy-start(f32[2,17,256]{2,1,0:T(8,128)} %constant.20.clone.twist_ref) | copy-start | bytes 104452
  46.3 3.9 %copy-start.7 = (s32[256]{0:T(256)S(1)}, s32[256]{0:T(256)}, u32[]{:S(2)}) copy-start(s32[256]{0:T(256)} %reshape.15.j_ref) | copy-start | bytes 3076
  50.3 1.6 %copy-start.1 = (f32[256,8,256]{2,1,0:T(8,128)S(1)}, f32[256,8,256]{2,1,0:T(8,128)}, u32[]{:S(2)}) copy-start(f32[256,8,256]{2,1,0:T(8,128)} %accumulate.1.owned_ref) | copy-start | bytes 6291460

commit v3 on v1

v3 whole, which is shorter than its diff:
```python
import functools
import math

import jax
import jax.numpy as jnp
import numpy as np
from jax import lax
from jax.experimental import pallas as pl
from jax.experimental.pallas import tpu as pltpu
from jax.sharding import PartitionSpec as P

NPHI = 8192
TR = 32
NJ = 256
TP = 256
PPS = 1024
COLS = 32
SLOTS_DEV = 64
HALF = COLS // 2 + 1
HALF_TP = TP // 2

F32 = jnp.float32
BF16 = jnp.bfloat16
CONTRACT_LAST = (((1,), (1,)), ((), ()))


def split(x):
    high = x.astype(BF16)
    return high, (x - high.astype(F32)).astype(BF16)


def place(taps, start):
    count = taps.shape[1]
    row = lax.broadcasted_iota(jnp.int32, (8, count), 0)
    starts = jnp.broadcast_to(start, (8, count))
    for bit in (1, 2, 4):
        taps = jnp.where((starts & bit) != 0, pltpu.roll(taps, bit, 0), taps)
    return taps, (starts - row + 7) >> 3


def expand(parts, group, groups, first=0):
    group = group.astype(F32)
    count = group.shape[1]
    pair = jnp.concatenate([group, group - 1.0], 0).astype(BF16)
    doubled = [jnp.concatenate([part.astype(F32)] * 2, 0).astype(BF16) for part in parts]
    zero = jnp.zeros((16, count), BF16)
    rows = [[] for _ in parts]
    for index in range(groups // 2):
        mask = pair == jnp.asarray(2 * index + first, BF16)
        for out, part in zip(rows, doubled):
            out.append(jnp.where(mask, part, zero))
    return [jnp.concatenate(out, 0) for out in rows]


MESH = pl.DeviceIdType.MESH
TILES = 4
FAR_FIRST = (2, 1, 3, 0)
STEPS = COLS // 4
SELF_STEP = 5


def spread_tile(half, values, cycle_taps, phi_taps, cycle_start, phi_start):
    cycle, cycle_group = place(cycle_taps * values, cycle_start)
    phi, phi_group = place(phi_taps, phi_start)
    cycle_high, cycle_low = expand(split(cycle), cycle_group, TR // 8)
    phi_high, phi_low = expand(split(phi), phi_group, HALF_TP // 8, half * (HALF_TP // 8))
    stacked = jnp.concatenate([cycle_high, cycle_low], 0)
    first = lax.dot_general(phi_high, stacked, CONTRACT_LAST, preferred_element_type=F32)
    second = lax.dot_general(phi_low, cycle_high, CONTRACT_LAST, preferred_element_type=F32)
    return (first[:, :TR] + first[:, TR:] + second).T


def read_tile(tile, cycle_taps, phi_taps, cycle_start, phi_start):
    tile_high, tile_low = split(tile)
    cycle, cycle_group = place(cycle_taps, cycle_start)
    phi, phi_group = place(phi_taps, phi_start)
    cycle_high, cycle_low = expand(split(cycle), cycle_group, TR // 8)
    right = jnp.concatenate([cycle_high, cycle_low, cycle_high], 0)
    left = jnp.concatenate([tile_high, tile_high, tile_low], 0).T
    along = jnp.dot(left, right, preferred_element_type=F32)
    picked = jnp.zeros((8, PPS), F32)
    for g in range(TP // 8):
        picked = jnp.where(phi_group == g, along[8 * g : 8 * g + 8], picked)
    return jnp.sum(picked * phi, 0, keepdims=True)


class Place:
    def __init__(self):
        self.column = lax.axis_index("pts")
        self.part = lax.axis_index("tile")
        z, self.y = self.column // 8, lax.rem(self.column // 2, 4)
        self.core = lax.rem(self.column, 2)
        self.ahead = [lax.rem(z + dz, 4) * 8 for dz in FAR_FIRST]
        self.behind = [lax.rem(z + 4 - dz, 4) * 8 for dz in FAR_FIRST]
        self.parts = [lax.rem(self.part + dx, 4) for dx in FAR_FIRST]

    def core_at(self, step):
        return lax.rem(self.core + 1 + step // 4, 2)

    def target(self, step, n):
        return self.ahead[n] + 2 * lax.rem(self.y + step + n, 4) + self.core_at(step)

    def source(self, step, n):
        return self.behind[n] + 2 * lax.rem(self.y + 16 - step - n, 4) + self.core_at(step)


def unless_self(step, n, action):
    if n != 3:
        action()
    elif isinstance(step, int):
        if step != SELF_STEP:
            action()
    else:
        pl.when(step != SELF_STEP)(action)


def greet(here):
    barrier = pltpu.get_barrier_semaphore()
    for step in range(STEPS):
        for n in range(4):
            column = here.target(step, n)
            for dx, part in zip(FAR_FIRST, here.parts):
                if (step, n, dx) != (SELF_STEP, 3, 0):
                    pl.semaphore_signal(
                        barrier, inc=1, device_id=(column, part), device_id_type=MESH
                    )
    return barrier


def bytes_of(ref, sem):
    return pltpu.make_async_copy(ref, ref, sem)


def times(re, im, cos, sin):
    return re * cos - im * sin, re * sin + im * cos


def turn(re, im, angle):
    cos, sin = math.cos(angle), math.sin(angle)
    if abs(sin) < 1e-12:
        return (re, im) if cos > 0 else (-re, -im)
    if abs(cos) < 1e-12:
        return (-im, re) if sin > 0 else (im, -re)
    return re * cos - im * sin, re * sin + im * cos


def real_fft(x):
    n = len(x)
    if n == 1:
        return [(x[0], None)]
    if n == 2:
        return [(x[0] + x[1], None), (x[0] - x[1], None)]
    even, odd = real_fft(x[0::2]), real_fft(x[1::2])
    out = [None] * (n // 2 + 1)
    out[0] = (even[0][0] + odd[0][0], None)
    out[n // 2] = (even[0][0] - odd[0][0], None)
    for k in range(1, n // 4):
        er, ei = even[k]
        tr, ti = turn(odd[k][0], odd[k][1], -2.0 * math.pi * k / n)
        out[k] = (er + tr, ei + ti)
        out[n // 2 - k] = (er - tr, ti - ei)
    quarter = n // 4
    out[quarter] = (even[quarter][0], -odd[quarter][0])
    return out


def real_inverse(spec):
    half = len(spec) - 1
    n = 2 * half
    if n == 2:
        return [spec[0][0] + spec[1][0], spec[0][0] - spec[1][0]]
    even, odd = [None] * (half // 2 + 1), [None] * (half // 2 + 1)
    even[0] = (spec[0][0] + spec[half][0], None)
    odd[0] = (spec[0][0] - spec[half][0], None)
    for k in range(1, half // 2):
        ar, ai = spec[k]
        br, bi = spec[half - k]
        even[k] = (ar + br, ai - bi)
        odd[k] = turn(ar - br, ai + bi, 2.0 * math.pi * k / n)
    middle = half // 2
    even[middle] = (2.0 * spec[middle][0], None)
    odd[middle] = (-2.0 * spec[middle][1], None)
    out = [None] * n
    out[0::2] = real_inverse(even)
    out[1::2] = real_inverse(odd)
    return out


def times_table(rows, table_high, table_low):
    high, low = split(rows)
    dot = functools.partial(jnp.dot, preferred_element_type=F32)
    return dot(high, table_high) + dot(high, table_low) + dot(low, table_high)


def filter_rows(rows, gain_ref, twist_ref, tables):
    cycles = rows[0].shape[0]
    spec = real_fft(rows)
    reals, imags = [], []
    for k in range(HALF):
        cos, sin = twist_ref[0, k : k + 1, :], twist_ref[1, k : k + 1, :]
        re, im = spec[k]
        if im is None:
            reals.append(re * cos)
            imags.append(-re * sin)
        else:
            re, im = times(re, im, cos, -sin)
            reals.append(re)
            imags.append(im)
    count = HALF * cycles
    both = times_table(jnp.concatenate(reals + imags, 0), tables[0], tables[1])
    first, last = both[:count], both[count:]
    freq_re = first[:, :TP] + last[:, TP:]
    freq_im = last[:, :TP] - first[:, TP:]
    gains = [jnp.broadcast_to(gain_ref[k : k + 1, :], (cycles, TP)) for k in range(HALF)]
    gain = jnp.concatenate(gains, 0)
    both = times_table(
        jnp.concatenate([freq_re * gain, freq_im * gain], 0), tables[2], tables[3]
    )
    first, last = both[:count], both[count:]
    back_re = first[:, :TP] - last[:, TP:]
    back_im = last[:, :TP] + first[:, TP:]
    spec = []
    for k in range(HALF):
        cos, sin = twist_ref[0, k : k + 1, :], twist_ref[1, k : k + 1, :]
        re, im = back_re[k * cycles : (k + 1) * cycles], back_im[k * cycles : (k + 1) * cycles]
        spec.append(times(re, im, cos, sin))
    return real_inverse(spec)


def filter_tables():
    index = np.arange(TP)
    low_half = 4 * (np.arange(HALF_TP) % COLS) + np.arange(HALF_TP) // COLS
    order = np.concatenate([low_half, TP - 1 - low_half])
    angle = 2.0 * np.pi * (np.outer(index, order) % TP) / TP
    tables = []
    for cos, sin in [(np.cos(angle), np.sin(angle)), (np.cos(angle).T, np.sin(angle).T)]:
        table = np.concatenate([cos, sin], 1).astype(np.float32)
        high = table.astype(BF16)
        tables += [high, (table - high.astype(np.float32)).astype(BF16)]
    angle = 2.0 * np.pi * np.outer(np.arange(HALF), index) / NPHI
    return np.stack([np.cos(angle), np.sin(angle)]).astype(np.float32), np.stack(tables)


def gain_table(response_ref):
    rows = [response_ref[HALF_TP * s : HALF_TP * (s + 1)].reshape(1, HALF_TP) for s in range(COLS)]
    turned = jnp.concatenate(rows, 0).T
    grid = jnp.concatenate([turned[COLS * b : COLS * (b + 1)] for b in range(4)], 1)
    lane = lax.broadcasted_iota(jnp.int32, (8, HALF_TP), 1)
    zeroth = jnp.broadcast_to(grid[:1], (8, HALF_TP))
    ahead = jnp.where(
        lane < 3 * COLS, pltpu.roll(zeroth, 3 * COLS, 1), pltpu.roll(zeroth, 3 * COLS - 1, 1)
    )
    last = response_ref[NPHI // 2 : NPHI // 2 + 1].reshape(1, 1)
    ahead = jnp.where(lane == HALF_TP - 1, jnp.broadcast_to(last, (8, HALF_TP)), ahead)
    mirrored = [ahead[:1]] + [grid[COLS - k : COLS - k + 1] for k in range(1, HALF)]
    both = jnp.concatenate([grid[:HALF], jnp.concatenate(mirrored, 0)], 1)
    return both * (1.0 / NPHI)


def same_block_links(wanted):
    lane = lax.broadcasted_iota(jnp.int32, (HALF_TP, HALF_TP), 1)
    across = [jnp.broadcast_to(wanted[k : k + 1], (HALF_TP, HALF_TP)) for k in range(2)]
    down = [x.T for x in across]
    item = [2 * lax.broadcasted_iota(jnp.int32, (HALF_TP, HALF_TP), 0) + k for k in range(2)]

    def latest(matches):
        found = [
            jnp.max(jnp.where(match, item[k], -1), 0, keepdims=True)
            for k, match in enumerate(matches)
        ]
        found = jnp.maximum(found[0], found[1])
        return jnp.where(found < 0, NJ, found)

    links = []
    for k in range(2):
        here = 2 * lane + k
        links.append(
            latest([jnp.logical_and(down[n] == across[k], item[n] < here) for n in range(2)])
        )
    for half in range(2):
        links.append(latest([down[n] == lane + HALF_TP * half for n in range(2)]))
    return links


def within(entry):
    return jnp.minimum(jnp.maximum(entry, 0), NJ)


CHUNKS = 4
CHUNK_J = 2
GROUP_J = CHUNKS * CHUNK_J


def whole_kernel(
    list_smem, list_vmem, v_ref, ct_ref, pt_ref, cs_ref, ps_ref,
    response_ref, twist_ref, table_ref,
    filtered_ref, gradient_ref,
    links_vmem, links, gain_ref, stage, arrived0, arrived1, owned, rows0, rows1,
    ready, filtered0, filtered1, picked, returned,
    links_sem, out_sem, send_tile, recv_tile, own_tile,
    send_row, recv_row0, recv_row1, own_row, send_out, recv_out, own_out,
    send_pick, recv_pick, own_pick,
):
    here = Place()
    barrier = greet(here)
    column_me, part_me = here.column, here.part
    me = column_me * TILES + part_me
    arrived, filtered = (arrived0, arrived1), (filtered0, filtered1)
    others = COLS * TILES - 1

    def each_other(step, n, action):
        column = here.target(step, n)
        for dx, part in zip(FAR_FIRST, here.parts):
            send = functools.partial(action, column, part)
            if dx:
                send()
            else:
                unless_self(step, n, send)

    def each_column(action):
        def visit(step, carry):
            for n in range(4):
                unless_self(step, n, functools.partial(action, here.target(step, n)))
            return carry

        lax.fori_loop(0, STEPS, visit, 0)

    def remote(source, target, sent, received, column, part):
        pltpu.make_async_remote_copy(
            source, target, sent, received, device_id=(column, part), device_id_type=MESH
        ).start()

    for n, link in enumerate(same_block_links(list_vmem[column_me])):
        links_vmem[n : n + 1, :] = link
    gain_ref[...] = gain_table(response_ref)
    for half in range(2):
        arrived[half][NJ] = jnp.zeros((8, HALF_TP), F32)

    def compute(half, step):
        for n in range(4):
            column = here.target(step, n)
            for k in range(2):
                slot = 2 * column + k
                row = pl.ds(slot, 1)
                tile = spread_tile(
                    half, v_ref[row, :], ct_ref[slot], pt_ref[slot], cs_ref[row, :], ps_ref[row, :]
                )
                stage[half, pl.ds(column * TILES, TILES), k] = tile.reshape(TILES, 8, HALF_TP)

    def dispatch(half, step):
        def send(column, part):
            remote(
                stage.at[half, column * TILES + part],
                arrived[half].at[pl.ds(2 * me, 2)],
                send_tile,
                recv_tile.at[half],
                column,
                part,
            )

        for n in range(4):
            each_other(step, n, send)

    def own_tiles(half):
        return pltpu.make_async_copy(
            stage.at[half, me], arrived[half].at[pl.ds(2 * me, 2)], own_tile.at[half]
        )

    copy_links = pltpu.make_async_copy(links_vmem, links, links_sem)
    compute(0, 0)
    copy_links.start()
    pl.semaphore_wait(barrier, others)
    for half in range(2):

        def spread_step(step, carry):
            compute(half, step)
            dispatch(half, step - 1)
            return carry

        if half:
            compute(half, 0)
            dispatch(0, STEPS - 1)
            own_tiles(0).start()
        lax.fori_loop(1, STEPS, spread_step, 0)
    dispatch(1, STEPS - 1)
    own_tiles(1).start()
    copy_links.wait()

    for half in range(2):
        tiles = arrived[half]
        bytes_of(tiles.at[pl.ds(0, 2 * others)], recv_tile.at[half]).wait()
        own_tiles(half).wait()

        def add(b, carry):
            for k in range(2):
                tiles[2 * b + k] = tiles[2 * b + k] + tiles[within(links[k, b])]
            return carry

        lax.fori_loop(0, COLS * TILES, add, 0, unroll=4)

        def gather(column):
            first = column // 16
            for j in range(GROUP_J):
                entry = links[2 + first, (column - 16 * first) * GROUP_J + j]
                owned[half, column * GROUP_J + j] = tiles[within(entry)]

        if half == 0:

            def send_rows(column):
                remote(
                    owned.at[0, pl.ds(column * GROUP_J, GROUP_J)],
                    rows0.at[column_me],
                    send_row,
                    recv_row0,
                    column,
                    part_me,
                )

            def row_step(step, carry):
                for n in range(4):
                    gather(here.target(step, n))
                for n in range(4):
                    column = here.target(step - 1, n)
                    unless_self(step - 1, n, functools.partial(send_rows, column))
                return carry

            for n in range(4):
                gather(here.target(0, n))
            lax.fori_loop(1, STEPS, row_step, 0)
            for n in range(4):
                send_rows(here.target(STEPS - 1, n))
        else:

            def row_step(step, carry):
                for n in range(4):
                    gather(here.target(step, n))
                return carry

            lax.fori_loop(0, STEPS, row_step, 0)

            def send_chunk(chunk, carry):
                def send(column):
                    remote(
                        owned.at[1, pl.ds(column * GROUP_J + chunk * CHUNK_J, CHUNK_J)],
                        rows1.at[chunk, column_me],
                        send_row,
                        recv_row1.at[chunk],
                        column,
                        part_me,
                    )

                each_column(send)
                return carry

            lax.fori_loop(0, CHUNKS, send_chunk, 0)

    own_rows = [
        pltpu.make_async_copy(
            owned.at[0, pl.ds(column_me * GROUP_J, GROUP_J)], rows0.at[column_me], own_row.at[0]
        )
    ]
    for chunk in range(CHUNKS):
        own_rows.append(
            pltpu.make_async_copy(
                owned.at[1, pl.ds(column_me * GROUP_J + chunk * CHUNK_J, CHUNK_J)],
                rows1.at[chunk, column_me],
                own_row.at[1 + chunk],
            )
        )
    for copy in own_rows:
        copy.start()
    for copy in own_rows:
        copy.wait()
    bytes_of(rows0.at[pl.ds(0, COLS - 1)], recv_row0).wait()

    def chunk_rows(chunk):
        return pl.ds(column_me * GROUP_J + chunk * CHUNK_J, CHUNK_J)

    def own_ready(half, chunk):
        return pltpu.make_async_copy(
            ready.at[half, chunk, column_me],
            filtered[half].at[chunk_rows(chunk)],
            own_out.at[half, chunk],
        )

    def send_ready(half, chunk):
        def send(column):
            remote(
                ready.at[half, chunk, column],
                filtered[half].at[chunk_rows(chunk)],
                send_out,
                recv_out.at[half],
                column,
                part_me,
            )

        each_column(send)
        own_ready(half, chunk).start()

    def filter_chunk(chunk, carry):
        bytes_of(rows1.at[chunk, pl.ds(0, COLS - 1)], recv_row1.at[chunk]).wait()
        rows = []
        for q in range(COLS):
            left = rows0[q, pl.ds(chunk * CHUNK_J, CHUNK_J)].reshape(CHUNK_J * 8, HALF_TP)
            right = rows1[chunk, q].reshape(CHUNK_J * 8, HALF_TP)
            rows.append(jnp.concatenate([left, right], 1))
        rows = filter_rows(rows, gain_ref, twist_ref, [table_ref[n] for n in range(4)])
        for q in range(COLS):
            for half in range(2):
                piece = rows[q][:, half * HALF_TP : (half + 1) * HALF_TP]
                ready[half, chunk, q] = piece.reshape(CHUNK_J, 8, HALF_TP)

        @pl.when(chunk >= 2)
        def _():
            send_ready(1, chunk - 2)

        send_ready(0, chunk)
        return carry

    lax.fori_loop(0, CHUNKS, filter_chunk, 0)
    for chunk in range(CHUNKS - 2, CHUNKS):
        send_ready(1, chunk)

    for half in range(2):
        source = filtered[half]
        for chunk in range(CHUNKS):
            own_ready(half, chunk).wait()
        bytes_of(source.at[pl.ds(0, NJ - GROUP_J)], recv_out.at[half]).wait()
        pltpu.make_async_copy(
            source, filtered_ref.at[:, :, pl.ds(half * HALF_TP, HALF_TP)], out_sem.at[half]
        ).start()

        def pick(step):
            for n in range(4):
                column = here.target(step, n)
                for part in range(TILES):
                    block = column * TILES + part
                    for k in range(2):
                        picked[half, block, k] = source[list_smem[column_me, k, block]]

        def send_picked(column, part):
            remote(
                picked.at[half, column * TILES + part],
                returned.at[half, column_me, part_me],
                send_pick,
                recv_pick.at[half, column_me],
                column,
                part,
            )

        def pick_step(step, carry):
            pick(step)
            for n in range(4):
                each_other(step - 1, n, send_picked)
            return carry

        pick(0)
        lax.fori_loop(1, STEPS, pick_step, 0)
        for n in range(4):
            each_other(STEPS - 1, n, send_picked)
        own = pltpu.make_async_copy(
            picked.at[half, me], returned.at[half, column_me, part_me], own_pick.at[half]
        )
        own.start()
        own.wait()

    def read(step, carry):
        columns = [here.source(step, n) for n in range(4)]
        for column in columns:
            for half in range(2):

                @pl.when(column != column_me)
                def _():
                    bytes_of(returned.at[half, column], recv_pick.at[half, column]).wait()

                @pl.when(column == column_me)
                def _():
                    bytes_of(
                        returned.at[half, column, pl.ds(0, TILES - 1)], recv_pick.at[half, column]
                    ).wait()

        for column in columns:
            for k in range(2):
                slot = 2 * column + k
                row = pl.ds(slot, 1)
                sides = [returned[half, column, :, k].reshape(TR, HALF_TP) for half in range(2)]
                gradient_ref[row, :] = read_tile(
                    jnp.concatenate(sides, 1),
                    ct_ref[slot],
                    pt_ref[slot],
                    cs_ref[row, :],
                    ps_ref[row, :],
                )
        return carry

    lax.fori_loop(0, STEPS, read, 0)
    bytes_of(stage.at[:, pl.ds(0, others)], send_tile).wait()
    bytes_of(owned.at[:, pl.ds(0, NJ - GROUP_J)], send_row).wait()
    bytes_of(ready.at[:, :, pl.ds(0, COLS - 1)], send_out).wait()
    bytes_of(picked.at[:, pl.ds(0, others)], send_pick).wait()
    for half in range(2):
        pltpu.make_async_copy(
            filtered[half],
            filtered_ref.at[:, :, pl.ds(half * HALF_TP, HALF_TP)],
            out_sem.at[half],
        ).wait()


def per_device(values, cycle_taps, phi_taps, cycle_start, phi_start, tile_list, response):
    lists = jnp.transpose(tile_list, (1, 2, 0))
    twist, tables = filter_tables()
    vmem = pl.BlockSpec(memory_space=pltpu.VMEM)
    tile = (8, HALF_TP)
    dma = pltpu.SemaphoreType.DMA
    filtered, gradient = pl.pallas_call(
        whole_kernel,
        in_specs=[pl.BlockSpec(memory_space=pltpu.SMEM)] + [vmem] * 9,
        out_specs=(pl.BlockSpec(memory_space=pl.ANY), vmem),
        out_shape=(
            jax.ShapeDtypeStruct((NJ, 8, TP), F32),
            jax.ShapeDtypeStruct((SLOTS_DEV, PPS), F32),
        ),
        scratch_shapes=[
            pltpu.VMEM((8, HALF_TP), jnp.int32),
            pltpu.SMEM((8, HALF_TP), jnp.int32),
            pltpu.VMEM((HALF, TP), F32),
            pltpu.VMEM((2, COLS * TILES, 2) + tile, F32),
            pltpu.VMEM((NJ + 2,) + tile, F32),
            pltpu.VMEM((NJ + 2,) + tile, F32),
            pltpu.VMEM((2, NJ) + tile, F32),
            pltpu.VMEM((COLS, GROUP_J) + tile, F32),
            pltpu.VMEM((CHUNKS, COLS, CHUNK_J) + tile, F32),
            pltpu.VMEM((2, CHUNKS, COLS, CHUNK_J) + tile, F32),
            pltpu.VMEM((NJ,) + tile, F32),
            pltpu.VMEM((NJ,) + tile, F32),
            pltpu.VMEM((2, COLS * TILES, 2) + tile, F32),
            pltpu.VMEM((2, COLS, TILES, 2) + tile, F32),
            dma,
            dma((2,)),
            dma,
            dma((2,)),
            dma((2,)),
            dma,
            dma,
            dma((CHUNKS,)),
            dma((1 + CHUNKS,)),
            dma,
            dma((2,)),
            dma((2, CHUNKS)),
            dma,
            dma((2, COLS)),
            dma((2,)),
        ],
        compiler_params=pltpu.CompilerParams(
            collective_id=0, has_side_effects=True, vmem_limit_bytes=56 << 20
        ),
        name="whole",
    )(
        lists,
        lists,
        values[0],
        cycle_taps[0],
        phi_taps[0],
        cycle_start[0],
        phi_start[0],
        response,
        jnp.asarray(twist),
        jnp.asarray(tables),
    )
    return filtered, gradient[None]


def solution(mesh):
    return jax.shard_map(
        per_device,
        mesh=mesh,
        in_specs=(
            P(("pts", "tile"), None, None),
            P(("pts", "tile"), None, None, None),
            P(("pts", "tile"), None, None, None),
            P(("pts", "tile"), None, None),
            P(("pts", "tile"), None, None),
            P(),
            P(),
        ),
        out_specs=(P(None, "tile", "pts"), P(("pts", "tile"), None, None)),
        check_vma=False,
    )
```

time: 203 us -> 124 us (0.61)
  blocking collectives: 70.6 us -> 0 us
  Pallas kernels: 52.3 us -> 119 us
  waiting for transfers between devices: 57.1 us -> 0 us
  starting transfers between devices: 15.6 us -> 0 us
    all_to_all x2 -> x0, blocking collectives: 70.6 us -> none  [the longest x1 35.7 us: per_device(): lax.all_to_all(picked, ('pts', 'tile'), split_axis=0, concat_axis=0, tile...]
    pallas_call x5 -> x1, Pallas kernels: 52.3 us -> 119 us  [per_device(): pl.pallas_call(whole_kernel, in_specs=[pl.BlockSpec(memory_space=pltpu.SM...]
    all_to_all x2 -> x0, waiting for transfers between devices: 57.1 us -> none  [the longest x1 29.9 us: per_device(): lax.all_to_all(partial, ('pts', 'tile'), split_axis=0, concat_axis=0, til...]
    all_to_all x2 -> x0, starting transfers between devices: 15.6 us -> none  [the longest x1 11.5 us: per_device(): lax.all_to_all(partial, ('pts', 'tile'), split_axis=0, concat_axis=0, til...]
    unnamed x13 -> x4, local copies, waits for them, and re-layouts: 4.13 us -> 3.79 us
  transfers between devices with their start and end apart: 2 -> 0, of which waited for: 2 -> 0; matrix products, arithmetic and copies ran while one was open for 1% -> 0% of each run, Pallas kernels for 0% -> 0%
where the time goes in v3:
time: 124 us; the launch traced here: 123 us
  Pallas kernels  119 us (96%)
  local copies, waits for them, and re-layouts  3.79 us (3%)
    pallas_call x1, Pallas kernels, per_device(): pl.pallas_call(whole_kernel, in_specs=[pl.BlockSpec(memory_space=pltpu.SM...  119 us
    unnamed x4, local copies, waits for them, and re-layouts  3.79 us

profile of v3, /device:TPU:1, one launch (start us, length us, event | category | flops | bytes accessed | tf_op | source)
XLA Modules:
  0.0 123.4 jit_solution(7229184043382041336)
XLA Ops:
  0.6 118.9 %whole.1 = (f32[256,8,256]{2,1,0:T(8,128)}, f32[64,1024]{1,0:T(8,128)}) custom-call(s32[32,2,128]{2,1,0:T(2,128)} %bitcast.13, s32[32,2,128]{2,1,0:T(2,128)} %bitcast.14, f32[64,1024]{1,0:T(8,128)} %bitcast.10, f32[64,8,1024]{2,1,0:T(8,128)} %bitcast.7, f32[64,8,1024]{2,1,0:T(8,128)} %bitcast.8, s32[64,1024]{1,0:T(8,128)} %bitcast.11, s32[64,1024]{1,0:T(8,128)} %bitcast.12, ...), custom_call_target="tpu_custom_call" | custom-call | tf_op jit(solution)/shard_map/whole/pallas_call | solution.py:615
  119.6 0.0 copy-start
  119.6 3.1 %copy.13 = f32[256,8,256]{2,1,0:T(8,128)} copy(f32[256,8,256]{2,1,0:T(8,128)} %get-tuple-element.8) | data formatting | bytes 4194304
  122.7 0.0 copy-done
  122.7 0.7 copy.14
Async XLA Ops:
  119.6 3.1 %copy-start = (f32[64,1024]{1,0:T(8,128)S(1)}, f32[64,1024]{1,0:T(8,128)}, u32[]{:S(2)}) copy-start(f32[64,1024]{1,0:T(8,128)} %get-tuple-element.5) | copy-start | bytes 786436

commit v4 on v3

--- a/solution.py
+++ b/solution.py
@@ -292,15 +292,33 @@
 
 
 def whole_kernel(
-    list_smem, list_vmem, v_ref, ct_ref, pt_ref, cs_ref, ps_ref,
-    response_ref, twist_ref, table_ref,
+    list_smem, list_vmem, v_hbm, ct_hbm, pt_hbm, cs_hbm, ps_hbm,
+    response_hbm, twist_hbm, table_hbm,
     filtered_ref, gradient_ref,
+    v_ref, ct_ref, pt_ref, cs_ref, ps_ref, response_ref, twist_ref, table_ref,
     links_vmem, links, gain_ref, stage, arrived0, arrived1, owned, rows0, rows1,
     ready, filtered0, filtered1, picked, returned,
-    links_sem, out_sem, send_tile, recv_tile, own_tile,
+    load_sem, links_sem, out_sem, send_tile, recv_tile, own_tile,
     send_row, recv_row0, recv_row1, own_row, send_out, recv_out, own_out,
     send_pick, recv_pick, own_pick,
 ):
+    loads = [
+        pltpu.make_async_copy(source, target, load_sem.at[n])
+        for n, (source, target) in enumerate(
+            [
+                (cs_hbm, cs_ref),
+                (ps_hbm, ps_ref),
+                (v_hbm, v_ref),
+                (ct_hbm, ct_ref),
+                (pt_hbm, pt_ref),
+                (response_hbm, response_ref),
+                (twist_hbm, twist_ref),
+                (table_hbm, table_ref),
+            ]
+        )
+    ]
+    for load in loads:
+        load.start()
     here = Place()
     barrier = greet(here)
     column_me, part_me = here.column, here.part
@@ -332,6 +350,8 @@
 
     for n, link in enumerate(same_block_links(list_vmem[column_me])):
         links_vmem[n : n + 1, :] = link
+    for load in loads[:6]:
+        load.wait()
     gain_ref[...] = gain_table(response_ref)
     for half in range(2):
         arrived[half][NJ] = jnp.zeros((8, HALF_TP), F32)
@@ -472,6 +492,8 @@
     for copy in own_rows:
         copy.wait()
     bytes_of(rows0.at[pl.ds(0, COLS - 1)], recv_row0).wait()
+    for load in loads[6:]:
+        load.wait()
 
     def chunk_rows(chunk):
         return pl.ds(column_me * GROUP_J + chunk * CHUNK_J, CHUNK_J)
@@ -610,17 +632,26 @@
     lists = jnp.transpose(tile_list, (1, 2, 0))
     twist, tables = filter_tables()
     vmem = pl.BlockSpec(memory_space=pltpu.VMEM)
+    hbm = pl.BlockSpec(memory_space=pltpu.HBM)
     tile = (8, HALF_TP)
     dma = pltpu.SemaphoreType.DMA
     filtered, gradient = pl.pallas_call(
         whole_kernel,
-        in_specs=[pl.BlockSpec(memory_space=pltpu.SMEM)] + [vmem] * 9,
+        in_specs=[pl.BlockSpec(memory_space=pltpu.SMEM), vmem] + [hbm] * 8,
         out_specs=(pl.BlockSpec(memory_space=pl.ANY), vmem),
         out_shape=(
             jax.ShapeDtypeStruct((NJ, 8, TP), F32),
             jax.ShapeDtypeStruct((SLOTS_DEV, PPS), F32),
         ),
         scratch_shapes=[
+            pltpu.VMEM(values.shape[1:], F32),
+            pltpu.VMEM(cycle_taps.shape[1:], F32),
+            pltpu.VMEM(phi_taps.shape[1:], F32),
+            pltpu.VMEM(cycle_start.shape[1:], jnp.int32),
+            pltpu.VMEM(phi_start.shape[1:], jnp.int32),
+            pltpu.VMEM(response.shape, F32),
+            pltpu.VMEM(twist.shape, F32),
+            pltpu.VMEM(tables.shape, BF16),
             pltpu.VMEM((8, HALF_TP), jnp.int32),
             pltpu.SMEM((8, HALF_TP), jnp.int32),
             pltpu.VMEM((HALF, TP), F32),
@@ -635,6 +666,7 @@
             pltpu.VMEM((NJ,) + tile, F32),
             pltpu.VMEM((2, COLS * TILES, 2) + tile, F32),
             pltpu.VMEM((2, COLS, TILES, 2) + tile, F32),
+            dma((8,)),
             dma,
             dma((2,)),
             dma,
@@ -652,7 +684,7 @@
             dma((2,)),
         ],
         compiler_params=pltpu.CompilerParams(
-            collective_id=0, has_side_effects=True, vmem_limit_bytes=56 << 20
+            collective_id=0, has_side_effects=True, vmem_limit_bytes=57 << 20
         ),
         name="whole",
     )(

time: 124 us -> 120 us (0.968)
  Pallas kernels: 119 us -> 116 us
    pallas_call x1, Pallas kernels: 119 us -> 116 us  [per_device(): pl.pallas_call(whole_kernel, in_specs=[pl.BlockSpec(memory_space=pltpu.SM...]
where the time goes in v4:
time: 120 us
  Pallas kernels  116 us (97%)
  local copies, waits for them, and re-layouts  3.79 us (3%)
    pallas_call x1, Pallas kernels, per_device(): pl.pallas_call(whole_kernel, in_specs=[pl.BlockSpec(memory_space=pltpu.SM...  116 us
    unnamed x4, local copies, waits for them, and re-layouts  3.79 us

profile of v4, /device:TPU:1, one launch (start us, length us, event | category | flops | bytes accessed | tf_op | source)
XLA Modules:
  0.0 120.2 jit_solution(4862019274007722553)
XLA Ops:
  0.6 115.7 %whole.1 = (f32[256,8,256]{2,1,0:T(8,128)}, f32[64,1024]{1,0:T(8,128)}) custom-call(s32[32,2,128]{2,1,0:T(2,128)} %bitcast.13, s32[32,2,128]{2,1,0:T(2,128)} %bitcast.14, f32[64,1024]{1,0:T(8,128)} %bitcast.10, f32[64,8,1024]{2,1,0:T(8,128)} %bitcast.7, f32[64,8,1024]{2,1,0:T(8,128)} %bitcast.8, s32[64,1024]{1,0:T(8,128)} %bitcast.11, s32[64,1024]{1,0:T(8,128)} %bitcast.12, ...), custom_call_target="tpu_custom_call" | custom-call | tf_op jit(solution)/shard_map/whole/pallas_call | solution.py:638
  116.4 0.0 copy-start
  116.4 3.1 %copy.13 = f32[256,8,256]{2,1,0:T(8,128)} copy(f32[256,8,256]{2,1,0:T(8,128)} %get-tuple-element.8) | data formatting | bytes 4194304
  119.4 0.0 copy-done
  119.5 0.7 copy.14
Async XLA Ops:
  116.4 3.1 %copy-start = (f32[64,1024]{1,0:T(8,128)S(1)}, f32[64,1024]{1,0:T(8,128)}, u32[]{:S(2)}) copy-start(f32[64,1024]{1,0:T(8,128)} %get-tuple-element.5) | copy-start | bytes 786436

commit v5 on v4

--- a/solution.py
+++ b/solution.py
@@ -348,14 +348,6 @@
             source, target, sent, received, device_id=(column, part), device_id_type=MESH
         ).start()
 
-    for n, link in enumerate(same_block_links(list_vmem[column_me])):
-        links_vmem[n : n + 1, :] = link
-    for load in loads[:6]:
-        load.wait()
-    gain_ref[...] = gain_table(response_ref)
-    for half in range(2):
-        arrived[half][NJ] = jnp.zeros((8, HALF_TP), F32)
-
     def compute(half, step):
         for n in range(4):
             column = here.target(step, n)
@@ -367,7 +359,7 @@
                 )
                 stage[half, pl.ds(column * TILES, TILES), k] = tile.reshape(TILES, 8, HALF_TP)
 
-    def dispatch(half, step):
+    def dispatch(half, step, members):
         def send(column, part):
             remote(
                 stage.at[half, column * TILES + part],
@@ -378,7 +370,7 @@
                 part,
             )
 
-        for n in range(4):
+        for n in members:
             each_other(step, n, send)
 
     def own_tiles(half):
@@ -386,24 +378,36 @@
             stage.at[half, me], arrived[half].at[pl.ds(2 * me, 2)], own_tile.at[half]
         )
 
-    copy_links = pltpu.make_async_copy(links_vmem, links, links_sem)
+    for load in loads[:5]:
+        load.wait()
     compute(0, 0)
-    copy_links.start()
     pl.semaphore_wait(barrier, others)
+    dispatch(0, 0, (0, 1, 2))
     for half in range(2):
 
         def spread_step(step, carry):
             compute(half, step)
-            dispatch(half, step - 1)
+            dispatch(half, step - 1, (3,))
+            dispatch(half, step, (0, 1, 2))
             return carry
 
         if half:
             compute(half, 0)
-            dispatch(0, STEPS - 1)
+            dispatch(0, STEPS - 1, (3,))
+            dispatch(1, 0, (0, 1, 2))
             own_tiles(0).start()
         lax.fori_loop(1, STEPS, spread_step, 0)
-    dispatch(1, STEPS - 1)
+
+    for n, link in enumerate(same_block_links(list_vmem[column_me])):
+        links_vmem[n : n + 1, :] = link
+    dispatch(1, STEPS - 1, (3,))
     own_tiles(1).start()
+    for half in range(2):
+        arrived[half][NJ] = jnp.zeros((8, HALF_TP), F32)
+    loads[5].wait()
+    gain_ref[...] = gain_table(response_ref)
+    copy_links = pltpu.make_async_copy(links_vmem, links, links_sem)
+    copy_links.start()
     copy_links.wait()
 
     for half in range(2):
@@ -626,6 +630,46 @@
             filtered_ref.at[:, :, pl.ds(half * HALF_TP, HALF_TP)],
             out_sem.at[half],
         ).wait()
+
+
+PIECES = 4
+
+
+def finish_kernel(filtered_in, gradient_in, filtered_out, gradient_out, tiles, points, into, outof):
+    def pieces(source, target, sem):
+        rows = NJ // PIECES
+        copies = [pltpu.make_async_copy(source[1], target[1], sem.at[PIECES])]
+        for n in range(PIECES):
+            part = pl.ds(n * rows, rows)
+            copies.append(
+                pltpu.make_async_copy(source[0].at[part], target[0].at[part], sem.at[n])
+            )
+        return copies
+
+    staged = (tiles, points)
+    first = pieces((filtered_in, gradient_in), staged, into)
+    second = pieces(staged, (filtered_out, gradient_out), outof)
+    for copy in first:
+        copy.start()
+    for arrival, departure in zip(first, second):
+        arrival.wait()
+        departure.start()
+    for copy in second:
+        copy.wait()
+
+
+def finish(filtered, gradient):
+    anywhere = pl.BlockSpec(memory_space=pl.ANY)
+    shapes = tuple(jax.ShapeDtypeStruct(x.shape, F32) for x in (filtered, gradient))
+    return pl.pallas_call(
+        finish_kernel,
+        in_specs=[anywhere] * 2,
+        out_specs=(anywhere,) * 2,
+        out_shape=shapes,
+        scratch_shapes=[pltpu.VMEM(x.shape, F32) for x in (filtered, gradient)]
+        + [pltpu.SemaphoreType.DMA((PIECES + 1,))] * 2,
+        name="finish",
+    )(filtered, gradient)
 
 
 def per_device(values, cycle_taps, phi_taps, cycle_start, phi_start, tile_list, response):
@@ -699,6 +743,7 @@
         jnp.asarray(twist),
         jnp.asarray(tables),
     )
+    filtered, gradient = finish(filtered, gradient)
     return filtered, gradient[None]
 
 

time: 120 us -> 121 us (level)
  Pallas kernels: 116 us -> 120 us
  local copies, waits for them, and re-layouts: 3.79 us -> 0 us
    unnamed x4 -> x0, local copies, waits for them, and re-layouts: 3.79 us -> none
    pallas_call x0 -> x1, Pallas kernels: none -> 2.52 us  [finish(): pl.pallas_call(finish_kernel, in_specs=[anywhere] * 2, out_specs=(anywher...]
    pallas_call x1, Pallas kernels: 116 us -> 117 us  [per_device(): pl.pallas_call(whole_kernel, in_specs=[pl.BlockSpec(memory_space=pltpu.SM...]
where the time goes in v5:
time: 121 us
  Pallas kernels  120 us (99%)
    pallas_call x1, Pallas kernels, per_device(): pl.pallas_call(whole_kernel, in_specs=[pl.BlockSpec(memory_space=pltpu.SM...  117 us
    pallas_call x1, Pallas kernels, finish(): pl.pallas_call(finish_kernel, in_specs=[anywhere] * 2, out_specs=(anywher...  2.52 us

profile of v5, /device:TPU:1, one launch (start us, length us, event | category | flops | bytes accessed | tf_op | source)
XLA Modules:
  0.0 120.6 jit_solution(13285566448953372529)
XLA Ops:
  0.6 117.5 %whole.1 = (f32[256,8,256]{2,1,0:T(8,128)}, f32[64,1024]{1,0:T(8,128)}) custom-call(s32[32,2,128]{2,1,0:T(2,128)} %bitcast.12, s32[32,2,128]{2,1,0:T(2,128)} %bitcast.13, f32[64,1024]{1,0:T(8,128)} %bitcast.9, f32[64,8,1024]{2,1,0:T(8,128)} %bitcast.7, f32[64,8,1024]{2,1,0:T(8,128)} %bitcast.8, s32[64,1024]{1,0:T(8,128)} %bitcast.10, s32[64,1024]{1,0:T(8,128)} %bitcast.11, ...), custom_call_target="tpu_custom_call" | custom-call | tf_op jit(solution)/shard_map/whole/pallas_call | solution.py:682
  118.1 2.5 %finish.1 = (f32[256,8,256]{2,1,0:T(8,128)}, f32[64,1024]{1,0:T(8,128)}) custom-call(f32[256,8,256]{2,1,0:T(8,128)} %get-tuple-element.6.filtered_in, f32[64,1024]{1,0:T(8,128)} %get-tuple-element.7.gradient_in), custom_call_target="tpu_custom_call" | custom-call | tf_op jit(solution)/shard_map/finish/pallas_call | solution.py:664

commit v6 on v5

--- a/solution.py
+++ b/solution.py
@@ -348,6 +348,14 @@
             source, target, sent, received, device_id=(column, part), device_id_type=MESH
         ).start()
 
+    for n, link in enumerate(same_block_links(list_vmem[column_me])):
+        links_vmem[n : n + 1, :] = link
+    for load in loads[:6]:
+        load.wait()
+    gain_ref[...] = gain_table(response_ref)
+    for half in range(2):
+        arrived[half][NJ] = jnp.zeros((8, HALF_TP), F32)
+
     def compute(half, step):
         for n in range(4):
             column = here.target(step, n)
@@ -359,7 +367,7 @@
                 )
                 stage[half, pl.ds(column * TILES, TILES), k] = tile.reshape(TILES, 8, HALF_TP)
 
-    def dispatch(half, step, members):
+    def dispatch(half, step):
         def send(column, part):
             remote(
                 stage.at[half, column * TILES + part],
@@ -370,7 +378,7 @@
                 part,
             )
 
-        for n in members:
+        for n in range(4):
             each_other(step, n, send)
 
     def own_tiles(half):
@@ -378,36 +386,24 @@
             stage.at[half, me], arrived[half].at[pl.ds(2 * me, 2)], own_tile.at[half]
         )
 
-    for load in loads[:5]:
-        load.wait()
+    copy_links = pltpu.make_async_copy(links_vmem, links, links_sem)
     compute(0, 0)
+    copy_links.start()
     pl.semaphore_wait(barrier, others)
-    dispatch(0, 0, (0, 1, 2))
     for half in range(2):
 
         def spread_step(step, carry):
             compute(half, step)
-            dispatch(half, step - 1, (3,))
-            dispatch(half, step, (0, 1, 2))
+            dispatch(half, step - 1)
             return carry
 
         if half:
             compute(half, 0)
-            dispatch(0, STEPS - 1, (3,))
-            dispatch(1, 0, (0, 1, 2))
+            dispatch(0, STEPS - 1)
             own_tiles(0).start()
         lax.fori_loop(1, STEPS, spread_step, 0)
-
-    for n, link in enumerate(same_block_links(list_vmem[column_me])):
-        links_vmem[n : n + 1, :] = link
-    dispatch(1, STEPS - 1, (3,))
+    dispatch(1, STEPS - 1)
     own_tiles(1).start()
-    for half in range(2):
-        arrived[half][NJ] = jnp.zeros((8, HALF_TP), F32)
-    loads[5].wait()
-    gain_ref[...] = gain_table(response_ref)
-    copy_links = pltpu.make_async_copy(links_vmem, links, links_sem)
-    copy_links.start()
     copy_links.wait()
 
     for half in range(2):

time: 121 us -> 119 us (0.983)
  Pallas kernels: 120 us -> 118 us
    pallas_call x1, Pallas kernels: 117 us -> 116 us  [per_device(): pl.pallas_call(whole_kernel, in_specs=[pl.BlockSpec(memory_space=pltpu.SM...]
where the time goes in v6:
time: 119 us
  Pallas kernels  118 us (99%)
    pallas_call x1, Pallas kernels, per_device(): pl.pallas_call(whole_kernel, in_specs=[pl.BlockSpec(memory_space=pltpu.SM...  116 us
    pallas_call x1, Pallas kernels, finish(): pl.pallas_call(finish_kernel, in_specs=[anywhere] * 2, out_specs=(anywher...  2.52 us

profile of v6, /device:TPU:1, one launch (start us, length us, event | category | flops | bytes accessed | tf_op | source)
XLA Modules:
  0.0 118.9 jit_solution(6602020589176225386)
XLA Ops:
  0.6 115.7 %whole.1 = (f32[256,8,256]{2,1,0:T(8,128)}, f32[64,1024]{1,0:T(8,128)}) custom-call(s32[32,2,128]{2,1,0:T(2,128)} %bitcast.12, s32[32,2,128]{2,1,0:T(2,128)} %bitcast.13, f32[64,1024]{1,0:T(8,128)} %bitcast.9, f32[64,8,1024]{2,1,0:T(8,128)} %bitcast.7, f32[64,8,1024]{2,1,0:T(8,128)} %bitcast.8, s32[64,1024]{1,0:T(8,128)} %bitcast.10, s32[64,1024]{1,0:T(8,128)} %bitcast.11, ...), custom_call_target="tpu_custom_call" | custom-call | tf_op jit(solution)/shard_map/whole/pallas_call | solution.py:678
  116.4 2.5 %finish.1 = (f32[256,8,256]{2,1,0:T(8,128)}, f32[64,1024]{1,0:T(8,128)}) custom-call(f32[256,8,256]{2,1,0:T(8,128)} %get-tuple-element.6.filtered_in, f32[64,1024]{1,0:T(8,128)} %get-tuple-element.7.gradient_in), custom_call_target="tpu_custom_call" | custom-call | tf_op jit(solution)/shard_map/finish/pallas_call | solution.py:660
